TPU v7x, 32 devices: a whole 2x2x4 slice. The times are simulated.
32 devices in a mesh: grp: 4 (over x, core), mem: 4 (over z), pair: 2 (over y).
Axes of the slice: x: 2, y: 2, z: 4, core: 2. Of those that a mesh axis runs over, the one named last changes fastest.
Arguments:
- voltages: bfloat16 [1024, 2, 71680], P(('grp', 'mem'), 'pair'), may hold values from -6 to 6
- gain_table: float32 [64, 2, 1024], P(None, None, 'mem'), may hold values from -4.2 to 4.2
- gain_index: int32 [1024, 2], replicated, may hold values from 0 to 63
- cylinder_map: int32 [1024], replicated, may hold values from 0 to 1023, each once
- delays: int32 [32, 1024], replicated, may hold values from 0 to 31
- chan_map: int32 [1024], replicated, may hold values from 0 to 1023, each once
Outputs:
- dedispersed: float32 [2, 512, 32, 32], P('pair', ('grp', 'mem'))
Inputs may be any that keep to these rules, and one draw needn't show every extreme that they name: `cylinder_map`: each of 0 to 1023 appears once. `chan_map`: each of 0 to 1023 appears once.
All inputs are finite; a program needn't handle non-finite values.
Results may differ from a plain program's by a relative error of at most 0.011.
Values may be sent and summed in bfloat16 or wider, within the bound.
A program may use at most 128 MiB of HBM per device.

v0:
```python
import math

import jax
import jax.numpy as jnp
from jax import lax
from jax.sharding import PartitionSpec as P

NFFT = 2048
CHANS = 1024
TAPS = 4
CYL = 4
NS = 256
FEEDS = 1024
TIMES = 32


HIGHEST_PRECISION = lax.Precision.HIGHEST


def pfb_window(tap_count, length):
    offsets = jnp.arange(tap_count * length, dtype=jnp.float32) + 0.5
    shaped = jnp.sinc((offsets - tap_count * length / 2.0) / length)
    taper_term = 0.5 - 0.5 * jnp.cos(offsets * (2.0 * math.pi / (tap_count * length)))
    return (shaped * taper_term).reshape(tap_count, length)


def channel_table(length, start_col, columns):
    samples = jnp.arange(length, dtype=jnp.int32)[:, None]
    channels = start_col + jnp.arange(columns, dtype=jnp.int32)[None, :]
    turns_int = samples * channels % length
    angles = turns_int.astype(jnp.float32) * (2.0 * math.pi / length)
    return (jnp.cos(angles).astype(jnp.bfloat16), (-jnp.sin(angles)).astype(jnp.bfloat16))


def frame_signal(volt_rows, window):
    leading = volt_rows.shape[0]
    frames = volt_rows.reshape(leading, TIMES + TAPS - 1, NFFT).astype(jnp.float32)
    framed = frames[:, 0:TIMES] * window[0]
    for tap_index in range(1, TAPS):
        framed = framed + frames[:, tap_index : tap_index + TIMES] * window[tap_index]
    return framed.astype(jnp.bfloat16).reshape(leading * TIMES, NFFT)


def beam_table(length):
    samples = jnp.arange(length, dtype=jnp.int32).reshape(length, 1, 1)
    beam_index = (
        jnp.arange(length, dtype=jnp.int32).reshape(length // 2, 2).T.reshape(1, 2, length // 2)
    )
    turns_int = samples * beam_index % length
    angles = turns_int.astype(jnp.float32) * (2.0 * math.pi / length)
    cosine = jnp.cos(angles).astype(jnp.bfloat16)
    sine_part = jnp.sin(angles).astype(jnp.bfloat16)
    first_row = jnp.stack([cosine, -sine_part], axis=1)
    second_row = jnp.stack([sine_part, cosine], axis=1)
    return jnp.stack([first_row, second_row], axis=1)


def beam_power(ns_real, ns_imag, feed_total):
    cylinders = ns_real.shape[1]
    indices = jnp.arange(cylinders, dtype=jnp.int32)
    turns_int = indices[:, None] * indices[None, :] % cylinders
    angles = turns_int.astype(jnp.float32) * (2.0 * math.pi / cylinders)
    cosine = jnp.cos(angles)
    sine_table = jnp.sin(angles)
    beam_real = jnp.einsum(
        "ec,lchq->lehq", cosine, ns_real, precision=HIGHEST_PRECISION
    ) + jnp.einsum("ec,lchq->lehq", sine_table, ns_imag, precision=HIGHEST_PRECISION)
    beam_imag = jnp.einsum(
        "ec,lchq->lehq", cosine, ns_imag, precision=HIGHEST_PRECISION
    ) - jnp.einsum("ec,lchq->lehq", sine_table, ns_real, precision=HIGHEST_PRECISION)
    return (beam_real * beam_real + beam_imag * beam_imag) * (1.0 / feed_total)


def time_tables(length):
    indices = jnp.arange(length, dtype=jnp.int32)
    turns_int = indices[:, None] * indices[None, :] % length
    angles = turns_int.astype(jnp.float32) * (2.0 * math.pi / length)
    return (jnp.cos(angles), jnp.sin(angles))


def dedisperse(beam_data, delays, chan_map):
    beam_count = beam_data.shape[0]
    values = beam_data.astype(jnp.float32)
    centred = values - jnp.mean(values, axis=1, keepdims=True)
    cosine, sine_table = time_tables(TIMES)
    spec_real = jnp.einsum("btc,tk->bkc", centred, cosine, precision=HIGHEST_PRECISION).astype(
        jnp.bfloat16
    )
    spec_imag = (
        -jnp.einsum("btc,tk->bkc", centred, sine_table, precision=HIGHEST_PRECISION)
    ).astype(jnp.bfloat16)
    trial_delay = jnp.take(delays, chan_map, axis=1)
    block_waves = 8

    def trial_block(start_wave):
        wave_index = start_wave + jnp.arange(block_waves, dtype=jnp.int32)
        turns_int = wave_index[:, None, None] * trial_delay[None] % TIMES
        angles = turns_int.astype(jnp.float32) * (2.0 * math.pi / TIMES)
        phase_real = jnp.cos(angles).astype(jnp.bfloat16)
        phase_imag = (-jnp.sin(angles)).astype(jnp.bfloat16)
        part_real = lax.dynamic_slice_in_dim(spec_real, start_wave, block_waves, 1)
        part_imag = lax.dynamic_slice_in_dim(spec_imag, start_wave, block_waves, 1)
        trial_real = jnp.einsum(
            "bkc,kjc->bkj", part_real, phase_real, preferred_element_type=jnp.float32
        ) - jnp.einsum("bkc,kjc->bkj", part_imag, phase_imag, preferred_element_type=jnp.float32)
        trial_imag = jnp.einsum(
            "bkc,kjc->bkj", part_real, phase_imag, preferred_element_type=jnp.float32
        ) + jnp.einsum("bkc,kjc->bkj", part_imag, phase_real, preferred_element_type=jnp.float32)
        return (trial_real, trial_imag)

    starts = jnp.arange(0, TIMES, block_waves, dtype=jnp.int32)
    trial_real, trial_imag = lax.map(trial_block, starts)
    trial_count = trial_real.shape[-1]
    trial_real = jnp.moveaxis(trial_real, 0, 1).reshape(beam_count, TIMES, trial_count)
    trial_imag = jnp.moveaxis(trial_imag, 0, 1).reshape(beam_count, TIMES, trial_count)
    scale_out = 1.0 / (TIMES * math.sqrt(CHANS))
    series = jnp.einsum(
        "bkj,kt->bjt", trial_real, cosine, precision=HIGHEST_PRECISION
    ) - jnp.einsum("bkj,kt->bjt", trial_imag, sine_table, precision=HIGHEST_PRECISION)
    return series * scale_out


def local(voltages, gain_table, gain_index, cylinder_map, delays, chan_map):
    local_feeds = voltages.shape[0]
    window = pfb_window(TAPS, NFFT)
    framed = frame_signal(voltages.reshape(local_feeds, voltages.shape[2]), window)
    scale_dft = 1.0 / math.sqrt(NFFT)
    block_cols = min(256, CHANS)

    def fill_block(block_index, spectra):
        start_col = block_index * block_cols
        cos_table, sin_table = channel_table(NFFT, start_col, block_cols)
        real_part = jnp.dot(framed, cos_table, preferred_element_type=jnp.float32) * scale_dft
        imag_part = jnp.dot(framed, sin_table, preferred_element_type=jnp.float32) * scale_dft
        stacked = jnp.stack([real_part, imag_part], axis=0).astype(jnp.bfloat16)
        stacked = stacked.reshape(2, local_feeds, TIMES, block_cols)
        return lax.dynamic_update_slice_in_dim(spectra, stacked, start_col, 3)

    spectra = lax.fori_loop(
        0, CHANS // block_cols, fill_block, jnp.zeros((2, local_feeds, TIMES, CHANS), jnp.bfloat16)
    )
    grp_count = lax.axis_size("grp")
    mem_count = lax.axis_size("mem")
    owners = cylinder_map // local_feeds
    slot_rows = (
        owners % mem_count * grp_count + owners // mem_count
    ) * local_feeds + cylinder_map % local_feeds
    table_beams = beam_table(NS)
    half_beams = CYL * (NS // 2)
    received = lax.all_to_all(
        lax.all_to_all(spectra, "grp", split_axis=2, concat_axis=1, tiled=True),
        "mem",
        split_axis=3,
        concat_axis=1,
        tiled=True,
    )
    polarization = lax.axis_index("pair")
    gain_column = lax.dynamic_index_in_dim(gain_index, polarization, 1, keepdims=False)
    gain_values = jnp.take(gain_table, jnp.take(gain_column, cylinder_map), axis=0)
    gain_real = gain_values[:, 0][:, None, :]
    gain_imag = gain_values[:, 1][:, None, :]
    ordered = jnp.take(received, slot_rows, axis=1)
    volt_real = ordered[0].astype(jnp.float32)
    volt_imag = ordered[1].astype(jnp.float32)
    cal_real = volt_real * gain_real - volt_imag * gain_imag
    cal_imag = volt_real * gain_imag + volt_imag * gain_real
    cal_grid = jnp.stack([cal_real, cal_imag], axis=0).astype(jnp.bfloat16)
    frame_local = cal_grid.shape[2]
    chan_local = cal_grid.shape[3]
    cal_grid = cal_grid.reshape(2, CYL, NS, frame_local * chan_local)
    ns_beams = jnp.einsum(
        "rcnq,nrsah->sachq", cal_grid, table_beams, preferred_element_type=jnp.float32
    )
    powers = beam_power(ns_beams[0], ns_beams[1], FEEDS)
    summed = lax.psum_scatter(powers, "pair", scatter_dimension=0, tiled=True)
    intensity = summed.astype(jnp.bfloat16).reshape(half_beams, frame_local, chan_local)
    beam_data = lax.all_to_all(
        lax.all_to_all(intensity, "grp", split_axis=0, concat_axis=1, tiled=True),
        "mem",
        split_axis=0,
        concat_axis=2,
        tiled=True,
    )
    series = dedisperse(beam_data, delays, chan_map)
    return series[None]


def solution(mesh):
    return jax.shard_map(
        local,
        mesh=mesh,
        in_specs=(P(("grp", "mem"), "pair", None), P(None, None, "mem"), P(), P(), P(), P()),
        out_specs=P("pair", ("grp", "mem"), None, None),
        check_vma=False,
    )
```

profile of v0, /device:TPU:0, one launch (start us, length us, event | category | flops | bytes accessed | tf_op | source)
XLA Modules:
  0.0 966.5 jit_solution(392109306165076913)
XLA Ops:
  19.5 31.6 %fusion.50 = bf16[64,32,2048]{2,1,0:T(8,128)(2,1)} fusion(f32[64,35,2048]{2,1,0:T(8,128)} %reshape.199, f32[2048]{0:T(1024)S(1)} %get-tuple-element.263, f32[2048]{0:T(1024)S(1)} %get-tuple-element.264, f32[2048]{0:T(1024)S(1)} %get-tuple-element.265, f32[2048]{0:T(1024)S(1)} %get-tuple-element.262), kind=kLoop, calls=%fused_computation.75 | loop fusion | flops 33554432 | bytes 75530240 | tf_op jit(solution)/shard_map/convert_element_type | solution.py:41
  55.4 129.2 %while.29 = (s32[]{:T(128)}, bf16[2,64,32,1024]{3,1,0,2:T(8,128)(2,1)}, bf16[2048,2048]{1,0:T(8,128)(2,1)}, s32[]{:T(128)}, s32[]{:T(128)}, /*index=5*/s32[]{:T(128)}, s32[]{:T(128)}) while((s32[]{:T(128)}, bf16[2,64,32,1024]{3,1,0,2:T(8,128)(2,1)}, bf16[2048,2048]{1,0:T(8,128)(2,1)}, s32[]{:T(128)}, s32[]{:T(128)}, /*index=5*/s32[]{:T(128)}, ...), condition=%wide.region_1.2_spmd, body=%wide.region_0.1_spmd.sunk | while | flops 4314365952 | bytes 31460484 | solution.py:139
  55.4 13.2 %fusion.217 = bf16[2048,256]{0,1:T(8,128)(2,1)S(1)} fusion(bf16[2048,2048]{1,0:T(8,128)(2,1)} %get-tuple-element.353, s32[256]{0:T(256)S(1)} %iota_add_fusion.6), kind=kOutput, calls=%fused_computation.11.clone.1 | convolution fusion | flops 2156920832 | bytes 9438208 | tf_op jit(solution)/shard_map/while/body/eval_jaxpr/dot_general | solution.py:134
  69.2 13.2 %fusion.218 = bf16[2048,256]{0,1:T(8,128)(2,1)S(1)} fusion(bf16[2048,2048]{1,0:T(8,128)(2,1)} %get-tuple-element.353, s32[256]{0:T(256)S(1)} %iota_add_fusion.6), kind=kOutput, calls=%fused_computation.12.clone.1 | convolution fusion | flops 2156396544 | bytes 9438208 | tf_op jit(solution)/shard_map/while/body/eval_jaxpr/dot_general | solution.py:133
  87.8 13.2 %fusion.217 = bf16[2048,256]{0,1:T(8,128)(2,1)S(1)} fusion(bf16[2048,2048]{1,0:T(8,128)(2,1)} %get-tuple-element.353, s32[256]{0:T(256)S(1)} %iota_add_fusion.6), kind=kOutput, calls=%fused_computation.11.clone.1 | convolution fusion | flops 2156920832 | bytes 9438208 | tf_op jit(solution)/shard_map/while/body/eval_jaxpr/dot_general | solution.py:134
  101.5 13.2 %fusion.218 = bf16[2048,256]{0,1:T(8,128)(2,1)S(1)} fusion(bf16[2048,2048]{1,0:T(8,128)(2,1)} %get-tuple-element.353, s32[256]{0:T(256)S(1)} %iota_add_fusion.6), kind=kOutput, calls=%fused_computation.12.clone.1 | convolution fusion | flops 2156396544 | bytes 9438208 | tf_op jit(solution)/shard_map/while/body/eval_jaxpr/dot_general | solution.py:133
  120.1 13.2 %fusion.217 = bf16[2048,256]{0,1:T(8,128)(2,1)S(1)} fusion(bf16[2048,2048]{1,0:T(8,128)(2,1)} %get-tuple-element.353, s32[256]{0:T(256)S(1)} %iota_add_fusion.6), kind=kOutput, calls=%fused_computation.11.clone.1 | convolution fusion | flops 2156920832 | bytes 9438208 | tf_op jit(solution)/shard_map/while/body/eval_jaxpr/dot_general | solution.py:134
  133.8 13.2 %fusion.218 = bf16[2048,256]{0,1:T(8,128)(2,1)S(1)} fusion(bf16[2048,2048]{1,0:T(8,128)(2,1)} %get-tuple-element.353, s32[256]{0:T(256)S(1)} %iota_add_fusion.6), kind=kOutput, calls=%fused_computation.12.clone.1 | convolution fusion | flops 2156396544 | bytes 9438208 | tf_op jit(solution)/shard_map/while/body/eval_jaxpr/dot_general | solution.py:133
  152.4 13.2 %fusion.217 = bf16[2048,256]{0,1:T(8,128)(2,1)S(1)} fusion(bf16[2048,2048]{1,0:T(8,128)(2,1)} %get-tuple-element.353, s32[256]{0:T(256)S(1)} %iota_add_fusion.6), kind=kOutput, calls=%fused_computation.11.clone.1 | convolution fusion | flops 2156920832 | bytes 9438208 | tf_op jit(solution)/shard_map/while/body/eval_jaxpr/dot_general | solution.py:134
  166.1 13.2 %fusion.218 = bf16[2048,256]{0,1:T(8,128)(2,1)S(1)} fusion(bf16[2048,2048]{1,0:T(8,128)(2,1)} %get-tuple-element.353, s32[256]{0:T(256)S(1)} %iota_add_fusion.6), kind=kOutput, calls=%fused_computation.12.clone.1 | convolution fusion | flops 2156396544 | bytes 9438208 | tf_op jit(solution)/shard_map/while/body/eval_jaxpr/dot_general | solution.py:133
  184.6 101.4 %all_to_all.63 = bf16[2,64,32,1024]{3,1,0,2:T(8,128)(2,1)} all-to-all(bf16[2,64,32,1024]{3,1,0,2:T(8,128)(2,1)} %get-tuple-element.185), channel_id=1, replica_groups=mesh['grp'=4,'mem'=4,'pair'=2] {'grp'}, dimensions={2} | all-to-all | bytes 16777216 | tf_op jit(solution)/shard_map/all_to_all | solution.py:151
  297.9 13.4 %copy.115 = bf16[2,256,8,1024]{1,2,0,3:T(8,128)(2,1)} copy(bf16[2,256,8,1024]{3,2,1,0:T(8,128)(2,1)} %bitcast.164) | data formatting | bytes 16777216 | tf_op jit(solution)/shard_map/all_to_all | solution.py:151
  334.1 166.8 %all-to-all-done.1 = bf16[2,256,8,1024]{1,2,0,3:T(8,128)(2,1)} async-done(((bf16[2,256,8,1024]{1,2,0,3:T(8,128)(2,1)}), bf16[2,256,8,1024]{1,2,0,3:T(8,128)(2,1)}, u32[]{:S(2)}, u32[]{:S(2)}) %all-to-all-start.1) | async-done | bytes 8388640 | tf_op jit(solution)/shard_map/all_to_all | solution.py:150
  500.9 15.9 %copy.117 = bf16[2,4,256,8,256]{4,3,2,1,0:T(8,128)(2,1)} copy(bf16[2,4,256,8,256]{2,3,0,4,1:T(8,128)(2,1)} %bitcast.23) | data formatting | bytes 16777216 | tf_op jit(solution)/shard_map/all_to_all | solution.py:150
  516.8 13.0 %gather_fusion.1 = bf16[1024,2,8,256]{3,2,1,0:T(8,128)(2,1)} fusion(bf16[2,1024,8,256]{3,2,1,0:T(8,128)(2,1)} %bitcast.162, s32[1024]{0:T(1024)S(1)} %broadcast_clamp_fusion.1), kind=kCustom, calls=%fused_computation.1 | custom fusion | bytes 16781312 | tf_op jit(solution)/shard_map/jit(_take)/gather | solution.py:162
  555.8 13.7 %fusion.68 = f32[2,2,4,128,2048]{4,3,2,1,0:T(8,128)} fusion(bf16[1,4,256,2048]{3,2,0,1:T(8,128)(2,1)} %stack.49, bf16[1,4,256,2048]{3,2,0,1:T(8,128)(2,1)} %stack.48, bf16[256,1,2,2,128]{0,4,1,3,2:T(8,128)(2,1)S(1)} %get-tuple-element.261, bf16[256,1,2,2,128]{0,4,1,3,2:T(8,128)(2,1)S(1)} %get-tuple-element.260), kind=kOutput, calls=%fused_computation.105 | convolution fusion | flops 4312793088 | bytes 25690112 | tf_op jit(solution)/shard_map/rcnq,nrsah->sachq/dot_general | solution.py:171
  576.0 18.4 %fusion.60 = f32[2,128,2048,4]{2,3,1,0:T(4,128)} fusion(f32[2,4,128,2048]{3,2,1,0:T(8,128)S(1)} %get-tuple-element.255), kind=kOutput, calls=%fused_computation.97 | convolution fusion | flops 100663520 | bytes 16777216 | tf_op jit(solution)/shard_map/ec,lchq->lehq/dot_general | solution.py:68
  594.4 19.0 %fusion.62 = f32[2,128,2048,4]{2,3,1,0:T(4,128)} fusion(f32[2,4,128,2048]{3,2,1,0:T(8,128)S(1)} %get-tuple-element.255), kind=kOutput, calls=%fused_computation.99 | convolution fusion | flops 100663520 | bytes 16777216 | tf_op jit(solution)/shard_map/ec,lchq->lehq/dot_general | solution.py:67
  613.4 18.5 %fusion.64 = f32[2,128,2048,4]{2,3,1,0:T(4,128)} fusion(f32[2,4,128,2048]{3,2,1,0:T(8,128)S(1)} %get-tuple-element.254), kind=kOutput, calls=%fused_computation.101 | convolution fusion | flops 100663520 | bytes 16777216 | tf_op jit(solution)/shard_map/ec,lchq->lehq/dot_general | solution.py:70
  631.8 30.1 %multiply_bitcast_fusion = f32[2,4,128,2048]{3,1,2,0:T(4,128)} fusion(f32[2,128,2048,4]{2,3,1,0:T(4,128)} %fusion.60, f32[2,128,2048,4]{2,3,1,0:T(4,128)} %fusion.64, f32[2,128,2048,4]{2,3,1,0:T(4,128)} %fusion.62, f32[2,4,128,2048]{3,2,1,0:T(8,128)} %copy-done.2), kind=kOutput, calls=%fused_computation.96 | convolution fusion | flops 113246432 | bytes 41943040 | tf_op jit(solution)/shard_map/ec,lchq->lehq/dot_general | solution.py:65
  673.5 97.9 %reduce-scatter.2.cloned.1.call-done = f32[1,4,128,2048]{3,2,1,0:T(8,128)} async-done(((f32[2,4,128,2048]{3,2,1,0:T(8,128)}), f32[1,4,128,2048]{3,2,1,0:T(8,128)}) %reduce-scatter.2.cloned.1.call-update) | async-done | bytes 4194320 | tf_op jit(solution)/shard_map/reduce_scatter | solution.py:175
  774.6 28.2 %all_to_all.64 = bf16[512,8,256]{2,1,0:T(8,128)(2,1)S(1)} all-to-all(bf16[512,8,256]{2,1,0:T(8,128)(2,1)S(1)} %bitcast.169), channel_id=1, replica_groups=mesh['grp'=4,'mem'=4,'pair'=2] {'grp'}, dimensions={0} | all-to-all | bytes 4194304 | tf_op jit(solution)/shard_map/all_to_all | solution.py:178
  812.5 44.4 %all-to-all-done.3 = bf16[128,32,256]{2,1,0:T(8,128)(2,1)S(1)} async-done(((bf16[128,32,256]{2,1,0:T(8,128)(2,1)}), bf16[128,32,256]{2,1,0:T(8,128)(2,1)S(1)}, u32[]{:S(2)}, u32[]{:S(2)}) %all-to-all-start.3) | async-done | bytes 2097184 | tf_op jit(solution)/shard_map/all_to_all | solution.py:177
  867.4 88.8 %while.30 = (s32[]{:T(128)}, f32[4,32,8,32]{1,3,2,0:T(8,128)S(1)}, f32[4,32,8,32]{1,3,2,0:T(8,128)S(1)}, s32[4]{0:T(128)S(1)}, s32[32,1024]{1,0:T(8,128)S(1)}, /...) while((s32[]{:T(128)}, f32[4,32,8,32]{1,3,2,0:T(8,128)S(1)}, ...), condition=%wide.region_5.6_spmd, body=%wide.region_4.5_spmd.sunk | while | flops 83378192 | bytes 5309699 | solution.py:112
  (117 shorter events, 226.2 us)
Async XLA Ops:
  6.5 315.5 %copy-start = (f32[64,2,256]{2,1,0:T(2,128)S(1)}, f32[64,2,256]{2,1,0:T(2,128)}, u32[]{:S(2)}) copy-start(f32[64,2,256]{2,1,0:T(2,128)} %param.11) | copy-start | bytes 393220
  311.3 6.0 copy-start.8
  311.3 6.1 copy-start.6
  311.3 189.5 %all-to-all-start.1 = ((bf16[2,256,8,1024]{1,2,0,3:T(8,128)(2,1)}), bf16[2,256,8,1024]{1,2,0,3:T(8,128)(2,1)}, u32[]{:S(2)}, u32[]{:S(2)}) async-start(bf16[2,256,8,1024]{1,2,0,3:T(8,128)(2,1)} %copy.115), calls=%async_computation.1 | async-start | bytes 16777216 | tf_op jit(solution)/shard_map/all_to_all | solution.py:150
  317.1 454.2 %reduce-scatter.2.cloned.1.call-start = ((), (), s32[]{:S(2)}) async-start(), calls=%async_computation.5 | async-start | bytes 12582912 | tf_op jit(solution)/shard_map/reduce_scatter | solution.py:175
  576.0 37.4 %copy-start.2 = (f32[2,4,128,2048]{3,2,1,0:T(8,128)}, f32[2,4,128,2048]{3,2,1,0:T(8,128)S(1)}, u32[]{:S(2)}) copy-start(f32[2,4,128,2048]{3,2,1,0:T(8,128)S(1)} %get-tuple-element.254) | copy-start | bytes 25165828
  773.9 35.1 %copy-start.5 = (s32[32,1024]{1,0:T(8,128)S(1)}, s32[32,1024]{1,0:T(8,128)}, u32[]{:S(2)}) copy-start(s32[32,1024]{1,0:T(8,128)} %param.14) | copy-start | bytes 393220
  773.9 35.3 %copy-start.7 = (s32[1024]{0:T(1024)S(1)}, s32[1024]{0:T(1024)}, u32[]{:S(2)}) copy-start(s32[1024]{0:T(1024)} %param.15) | copy-start | bytes 12292
  804.4 52.4 %all-to-all-start.3 = ((bf16[128,32,256]{2,1,0:T(8,128)(2,1)}), bf16[128,32,256]{2,1,0:T(8,128)(2,1)S(1)}, u32[]{:S(2)}, u32[]{:S(2)}) async-start(bf16[128,32,256]{2,1,0:T(8,128)(2,1)} %bitcast.168), calls=%async_computation.4 | async-start | bytes 4194304 | tf_op jit(solution)/shard_map/all_to_all | solution.py:177
  857.4 10.0 %copy-start.3 = (f32[4,32,8,32]{1,3,2,0:T(8,128)S(1)}, f32[4,32,8,32]{1,3,2,0:T(8,128)}, u32[]{:S(2)}) copy-start(f32[4,32,8,32]{1,3,2,0:T(8,128)} %custom-call.8) | copy-start | bytes 393220
  857.4 10.0 %copy-start.4 = (f32[4,32,8,32]{1,3,2,0:T(8,128)S(1)}, f32[4,32,8,32]{1,3,2,0:T(8,128)}, u32[]{:S(2)}) copy-start(f32[4,32,8,32]{1,3,2,0:T(8,128)} %custom-call.9) | copy-start | bytes 393220
  956.2 3.2 copy-start.1
Sparse Core Ops, SparseCore 0:
  673.6 97.7 reduce-scatter.1
where the time goes:
time: 977 us; the launch traced here: 966 us
  waiting for transfers between devices  309 us (32%)
  matrix products  286 us (29%)
  local copies, waits for them, and re-layouts  148 us (15%)
  blocking collectives  130 us (13%)
  other arithmetic  60.5 us (6%)
  between operations  13.9 us (1%)
  starting transfers between devices  10.6 us (1%)
    all_to_all x1, waiting for transfers between devices, local(): lax.all_to_all(lax.all_to_all(spectra, 'grp', split_axis=2, concat_axis=1...  167 us
    all_to_all x1, blocking collectives, local(): lax.all_to_all(spectra, 'grp', split_axis=2, concat_axis=1, tiled=True)  101 us
    reduce_scatter x1, waiting for transfers between devices, local(): summed = lax.psum_scatter(powers, 'pair', scatter_dimension=0, tiled=True)  97.9 us
    dot_general x4, matrix products, fill_block(): jnp.dot(framed, cos_table, preferred_element_type=jnp.float32) * scale_dft  53 us
    dot_general x4, matrix products, fill_block(): jnp.dot(framed, sin_table, preferred_element_type=jnp.float32) * scale_dft  52.8 us
    all_to_all x1, waiting for transfers between devices, local(): lax.all_to_all(lax.all_to_all(intensity, 'grp', split_axis=0, concat_axis...  44.4 us
    convert_element_type x1, other arithmetic, frame_signal(): return framed.astype(jnp.bfloat16).reshape(leading * TIMES, NFFT)  31.6 us
    dot_general x1, matrix products, beam_power(): jnp.einsum('ec,lchq->lehq', cosine, ns_real, precision=HIGHEST_PRECISION)  30.1 us
  transfers between devices with their start and end apart: 3, of which 3 were waited for; matrix products, arithmetic and copies ran while one was open for 2% of the time, Pallas kernels for 0%

commit v1 on v0

v1 whole, which is shorter than its diff:
```python
import functools
import math

import jax
import jax.numpy as jnp
from jax import lax
from jax.experimental import pallas as pl
from jax.experimental.pallas import tpu as pltpu
from jax.sharding import PartitionSpec as P

NFFT = 2048
CHANS = 1024
TAPS = 4
CYL = 4
NS = 256
FEEDS = 1024
BEAMS = 1024
TIMES = 32
TRIALS = 32
PEERS = ("grp", "mem")
LANES = 128


def pfb_window(tap_count, length):
    offsets = jnp.arange(tap_count * length, dtype=jnp.float32) + 0.5
    shaped = jnp.sinc((offsets - tap_count * length / 2.0) / length)
    taper_term = 0.5 - 0.5 * jnp.cos(offsets * (2.0 * math.pi / (tap_count * length)))
    return (shaped * taper_term).reshape(tap_count, length)


def turn(index, length):
    angles = (index % length).astype(jnp.float32) * (2.0 * math.pi / length)
    return lax.optimization_barrier((jnp.cos(angles), jnp.sin(angles)))


def times(a, b):
    return (a[0] * b[0] - a[1] * b[1], a[0] * b[1] + a[1] * b[0])


def channel_table(chan_of, quarter):
    chan = chan_of[None, :]
    high = turn(jnp.arange(16, dtype=jnp.int32)[:, None] * 128 * chan, NFFT)
    mid = turn(jnp.arange(16, dtype=jnp.int32)[:, None] * 8 * chan, NFFT)
    low = turn(jnp.arange(8, dtype=jnp.int32)[:, None] * chan + quarter[None, :] * (NFFT // 4), NFFT)
    upper = times([p[:, None, :] for p in high], [p[None, :, :] for p in mid])
    upper = lax.optimization_barrier(tuple(p.reshape(NFFT // 8, 1, -1) for p in upper))
    table = upper[0] * low[0][None] - upper[1] * low[1][None]
    return table.astype(jnp.bfloat16).reshape(NFFT, -1)


def beam_weights(cylinder_map):
    slots = jnp.arange(FEEDS, dtype=jnp.int32)
    hit = cylinder_map[:, None] == slots[None, :]
    slot_of = jnp.sum(jnp.where(hit, slots[:, None], 0), axis=0)
    cyl, pos = slot_of // NS, slot_of % NS
    e = jnp.arange(CYL, dtype=jnp.int32).reshape(CYL, 1, 1)
    hh = jnp.arange(16, dtype=jnp.int32).reshape(1, 16, 1)
    upper = turn(16 * pos * hh + (NS // CYL) * e * cyl, NS)
    a = jnp.arange(2, dtype=jnp.int32).reshape(2, 1, 1)
    hl = jnp.arange(8, dtype=jnp.int32).reshape(1, 8, 1)
    lower = turn(pos * (2 * hl + a), NS)
    real, imag = times(
        [p[None, :, :, None, :] for p in upper], [p[:, None, None, :, :] for p in lower]
    )
    return jnp.concatenate(
        [p.astype(jnp.bfloat16).reshape(BEAMS, FEEDS) for p in (real, imag)], axis=1
    )


def frame_signal(volt_rows, window):
    leading = volt_rows.shape[0]
    frames = volt_rows.reshape(leading, TIMES + TAPS - 1, NFFT).astype(jnp.float32)
    framed = frames[:, 0:TIMES] * window[0]
    for tap_index in range(1, TAPS):
        framed = framed + frames[:, tap_index : tap_index + TIMES] * window[tap_index]
    return framed.astype(jnp.bfloat16)


HIT = (TIMES - 1) / (TIMES * TIMES)
MISS = -1.0 / (TIMES * TIMES)


def beam_kernel(block, chans, r_ref, ga_ref, gb_ref, w_ref, e_ref, out_ref, x_ref, t_ref, p_ref):
    step = pl.program_id(0)
    width = 2 * chans
    lane = lax.broadcasted_iota(jnp.int32, (FEEDS, width), 1)
    sign = jnp.where(lane < chans, 1.0, -1.0)
    for i in range(block):
        volt = r_ref[:, i].reshape(FEEDS, width).astype(jnp.float32)
        cal = volt * ga_ref[...] + pltpu.roll(volt, chans, 1) * gb_ref[...]
        turned = pltpu.roll(cal, chans, 1) * sign
        cols = slice(i * width, (i + 1) * width)
        x_ref[0:FEEDS, cols] = cal.astype(jnp.bfloat16)
        x_ref[FEEDS : 2 * FEEDS, cols] = turned.astype(jnp.bfloat16)
        hit = e_ref[...] == step * block + i
        t_ref[i * chans : (i + 1) * chans, :] = jnp.where(hit, HIT, MISS).astype(jnp.bfloat16)
    low = lax.broadcasted_iota(jnp.int32, (BEAMS, width), 1) < chans
    for i in range(0, block, 2):
        cols = slice(i * width, (i + 2) * width)
        beams = jnp.dot(w_ref[...], x_ref[:, cols], preferred_element_type=jnp.float32)
        squares = beams * beams
        one, two = squares[:, :width], squares[:, width:]
        first = one + pltpu.roll(one, chans, 1)
        second = two + pltpu.roll(two, chans, 1)
        power = jnp.where(low, first, second) * (1.0 / FEEDS)
        p_ref[:, i * chans : (i + 2) * chans] = power.astype(jnp.bfloat16)
    part = jnp.dot(p_ref[...], t_ref[...], preferred_element_type=jnp.float32)

    @pl.when(step == 0)
    def _():
        out_ref[...] = part

    @pl.when(step > 0)
    def _():
        out_ref[...] += part


def beam_stage(received, gains, weights, shift):
    peers, _, feeds, width = received.shape
    chans = width // 2
    if width != LANES:
        volt = jnp.moveaxis(received, 1, 0).reshape(TIMES, FEEDS, 2, chans).astype(jnp.float32)
        ga, gb = (g.reshape(FEEDS, 2, chans) for g in gains)
        cal = (volt * ga + volt[:, :, ::-1] * gb).astype(jnp.bfloat16)
        turned = jnp.stack([cal[:, :, 1], -cal[:, :, 0]], axis=2)
        both = jnp.concatenate([cal, turned], axis=1)
        beams = jnp.einsum("bf,tfrc->btrc", weights, both, preferred_element_type=jnp.float32)
        power = jnp.sum(beams * beams, axis=2) * (1.0 / FEEDS)
        power = power.astype(jnp.bfloat16).reshape(BEAMS, TIMES * chans)
        hit = shift[None] == jnp.arange(TIMES, dtype=jnp.int32)[:, None, None]
        spread = jnp.where(hit, HIT, MISS).astype(jnp.bfloat16).reshape(TIMES * chans, -1)
        return jnp.dot(power, spread, preferred_element_type=jnp.float32)
    block = 8
    series = TRIALS * TIMES
    whole = lambda shape: pl.BlockSpec(shape, lambda i: (0,) * len(shape))
    return pl.pallas_call(
        functools.partial(beam_kernel, block, chans),
        grid=(TIMES // block,),
        out_shape=jax.ShapeDtypeStruct((BEAMS, series), jnp.float32),
        in_specs=[
            pl.BlockSpec((peers, block, feeds, width), lambda i: (0, i, 0, 0)),
            whole((FEEDS, width)),
            whole((FEEDS, width)),
            whole((BEAMS, 2 * FEEDS)),
            whole((chans, series)),
        ],
        out_specs=whole((BEAMS, series)),
        scratch_shapes=[
            pltpu.VMEM((2 * FEEDS, block * width), jnp.bfloat16),
            pltpu.VMEM((block * chans, series), jnp.bfloat16),
            pltpu.VMEM((BEAMS, block * chans), jnp.bfloat16),
        ],
        compiler_params=pltpu.CompilerParams(
            dimension_semantics=("arbitrary",), vmem_limit_bytes=60 * 1024 * 1024
        ),
    )(received, *gains, weights, shift)


def local(voltages, gain_table, gain_index, cylinder_map, delays, chan_map):
    feeds = voltages.shape[0]
    grp_count, mem_count = lax.axis_size("grp"), lax.axis_size("mem")
    peers = grp_count * mem_count
    chans = CHANS // peers
    grp, mem = lax.axis_index("grp"), lax.axis_index("mem")

    window = pfb_window(TAPS, NFFT)
    framed = frame_signal(voltages.reshape(feeds, voltages.shape[2]), window)
    peer = jnp.arange(peers, dtype=jnp.int32)
    base = peer % mem_count * (CHANS // mem_count) + peer // mem_count * chans
    chan_of = base[:, None, None] + jnp.arange(chans, dtype=jnp.int32)[None, None, :]
    quarter = jnp.arange(2, dtype=jnp.int32)[None, :, None]
    chan_of, quarter = (
        jnp.broadcast_to(v, (peers, 2, chans)).reshape(-1) for v in (chan_of, quarter)
    )
    table = channel_table(chan_of, quarter)

    rows = jnp.swapaxes(framed, 0, 1).reshape(TIMES * feeds, NFFT)
    spectra = jnp.dot(rows, table, preferred_element_type=jnp.float32) * (1.0 / math.sqrt(NFFT))
    spectra = spectra.astype(jnp.bfloat16).reshape(TIMES, feeds, peers, 2 * chans)
    spectra = jnp.moveaxis(spectra, 2, 0)
    received = lax.all_to_all(spectra, PEERS, split_axis=0, concat_axis=0, tiled=True)

    weights = beam_weights(cylinder_map)
    gain_here = lax.dynamic_slice_in_dim(gain_table, grp * chans, chans, 2)
    gain_rows = gain_index[:, lax.axis_index("pair")]
    pick = gain_rows[:, None] == jnp.arange(gain_table.shape[0], dtype=jnp.int32)[None, :]
    gain_values = jnp.dot(
        pick.astype(jnp.float32),
        gain_here.reshape(gain_table.shape[0], 2 * chans),
        precision=lax.Precision.HIGHEST,
    )
    gain_real, gain_imag = gain_values[:, :chans], gain_values[:, chans:]
    gains = (
        jnp.concatenate([gain_real, gain_real], axis=1),
        jnp.concatenate([-gain_imag, gain_imag], axis=1),
    )

    first = mem * (CHANS // mem_count) + grp * chans
    freq = lax.dynamic_slice_in_dim(chan_map, first, chans, 0)
    column = jnp.arange(CHANS, dtype=jnp.int32)[:, None] == freq[None, :]
    delay = jnp.dot(
        delays.astype(jnp.bfloat16), column.astype(jnp.bfloat16), preferred_element_type=jnp.float32
    ).astype(jnp.int32)
    frame = jnp.arange(TIMES, dtype=jnp.int32)[None, None, :]
    shift = ((frame - delay.T[:, :, None]) % TIMES).reshape(chans, TRIALS * TIMES)

    part = beam_stage(received, gains, weights, shift)

    pairs = lax.axis_size("pair")
    owned = BEAMS // (pairs * peers)
    part = part.astype(jnp.bfloat16).reshape(pairs * peers, owned, TRIALS * TIMES)
    parts = lax.all_to_all(part, ("pair",) + PEERS, split_axis=0, concat_axis=0, tiled=True)
    series = jnp.sum(parts.astype(jnp.float32), axis=0)
    return series.reshape(1, owned, TRIALS, TIMES)


def solution(mesh):
    return jax.shard_map(
        local,
        mesh=mesh,
        in_specs=(P(PEERS, "pair", None), P(None, None, "mem"), P(), P(), P(), P()),
        out_specs=P("pair", PEERS, None, None),
        check_vma=False,
    )
```

time: 977 us -> 377 us (0.39)
  matrix products: 286 us -> 22.8 us
  waiting for transfers between devices: 309 us -> 174 us
  local copies, waits for them, and re-layouts: 148 us -> 45.1 us
  blocking collectives: 130 us -> 50.6 us
  Pallas kernels: 0 us -> 30.5 us
  other arithmetic: 60.5 us -> 44.5 us
  between operations: 13.9 us -> 0.2 us
    dot_general x33 -> x3, matrix products: 286 us -> 22.8 us  [the longest x1 22.1 us: local(): jnp.dot(rows, table, preferred_element_type=jnp.float32)]
    reduce_scatter x1 -> x0, waiting for transfers between devices: 97.9 us -> none  [local(): summed = lax.psum_scatter(powers, 'pair', scatter_dimension=0, tiled=True)]
    all_to_all x2 -> x1, blocking collectives: 130 us -> 50.6 us  [local(): lax.all_to_all(part, ('pair',) + PEERS, split_axis=0, concat_axis=0, tile...]
    all_to_all x4 -> x0, local copies, waits for them, and re-layouts: 42.9 us -> none  [the longest x2 25.3 us: local(): lax.all_to_all(spectra, 'grp', split_axis=2, concat_axis=1, tiled=True)]
    all_to_all x2 -> x1, waiting for transfers between devices: 211 us -> 174 us  [local(): lax.all_to_all(spectra, PEERS, split_axis=0, concat_axis=0, tiled=True)]
    convert_element_type x3 -> x2, other arithmetic: 35.3 us -> 3.67 us  [the longest x1 2.51 us: local(): part.astype(jnp.bfloat16).reshape(pairs * peers, owned, TRIALS * TIMES)]
    transpose x0 -> x1, other arithmetic: none -> 31.6 us  [local(): rows = jnp.swapaxes(framed, 0, 1).reshape(TIMES * feeds, NFFT)]
    pallas_call x0 -> x1, Pallas kernels: none -> 30.5 us  [beam_stage(): pl.pallas_call(functools.partial(beam_kernel, block, chans), grid=(TIMES...]
  transfers between devices with their start and end apart: 3 -> 1, of which waited for: 3 -> 1; matrix products, arithmetic and copies ran while one was open for 2% -> 3% of each run, Pallas kernels for 0% -> 0%
where the time goes in v1:
time: 377 us; the launch traced here: 376 us
  waiting for transfers between devices  174 us (46%)
  blocking collectives  50.6 us (13%)
  local copies, waits for them, and re-layouts  45.1 us (12%)
  other arithmetic  44.5 us (12%)
  Pallas kernels  30.5 us (8%)
  matrix products  22.8 us (6%)
  starting transfers between devices  7.58 us (2%)
    all_to_all x1, waiting for transfers between devices, local(): lax.all_to_all(spectra, PEERS, split_axis=0, concat_axis=0, tiled=True)  174 us
    all_to_all x1, blocking collectives, local(): lax.all_to_all(part, ('pair',) + PEERS, split_axis=0, concat_axis=0, tile...  50.6 us
    transpose x1, other arithmetic, local(): rows = jnp.swapaxes(framed, 0, 1).reshape(TIMES * feeds, NFFT)  31.6 us
    pallas_call x1, Pallas kernels, beam_stage(): pl.pallas_call(functools.partial(beam_kernel, block, chans), grid=(TIMES...  30.5 us
    dot_general x1, matrix products, local(): jnp.dot(rows, table, preferred_element_type=jnp.float32)  22.1 us
    convert_element_type x1, local copies, waits for them, and re-layouts, frame_signal(): volt_rows.reshape(leading, TIMES + TAPS - 1, NFFT).astype(jnp.float32)  12.8 us
    transpose x1, local copies, waits for them, and re-layouts, local(): rows = jnp.swapaxes(framed, 0, 1).reshape(TIMES * feeds, NFFT)  11.2 us
    unnamed x9, local copies, waits for them, and re-layouts  9.77 us
  transfers between devices with their start and end apart: 1, of which 1 were waited for; matrix products, arithmetic and copies ran while one was open for 3% of the time, Pallas kernels for 0%

profile of v1, /device:TPU:0, one launch (start us, length us, event | category | flops | bytes accessed | tf_op | source)
XLA Modules:
  0.0 375.5 jit_solution(12138724838532175884)
XLA Ops:
  0.2 12.8 %reshape.377 = f32[64,35,2048]{2,1,0:T(8,128)} reshape(bf16[64,1,71680]{2,0,1:T(8,128)(2,1)} %param.6) | data formatting | bytes 27525120 | tf_op jit(solution)/shard_map/convert_element_type | solution.py:72
  13.0 31.6 %fusion.10 = bf16[32,64,2048]{2,0,1:T(8,128)(2,1)} fusion(f32[2048]{0:T(1024)S(1)} %get-tuple-element.39, f32[64,35,2048]{2,1,0:T(8,128)} %reshape.377, f32[2048]{0:T(1024)S(1)} %get-tuple-element.40, f32[2048]{0:T(1024)S(1)} %get-tuple-element.41, f32[2048]{0:T(1024)S(1)} %get-tuple-element.38), kind=kLoop, calls=%fused_computation.16 | loop fusion | flops 33554432 | bytes 75530240 | tf_op jit(solution)/shard_map/transpose | solution.py:177
  44.6 11.2 %copy.15 = bf16[32,64,2048]{2,1,0:T(8,128)(2,1)} copy(bf16[32,64,2048]{2,0,1:T(8,128)(2,1)} %fusion.10) | data formatting | bytes 16777216 | tf_op jit(solution)/shard_map/transpose | solution.py:177
  56.3 1.1 fusion.38
  57.4 0.6 multiply_add_fusion
  58.0 22.1 %fusion.11 = bf16[256,8,16,128]{3,1,2,0:T(8,128)(2,1)} fusion(bf16[2048,2048]{1,0:T(8,128)(2,1)} %bitcast.31, f32[8,2048]{1,0:T(8,128)S(1)} %get-tuple-element.24, f32[256,2048]{1,0:T(8,128)S(1)} %bitcast.34, f32[8,2048]{1,0:T(8,128)S(1)} %get-tuple-element.22, f32[256,2048]{1,0:T(8,128)S(1)} %bitcast.35), kind=kOutput, calls=%fused_computation.17 | convolution fusion | flops 17205035008 | bytes 21102592 | tf_op jit(solution)/shard_map/dot_general | solution.py:178
  80.2 9.8 %copy.21 = bf16[256,8,16,128]{3,2,1,0:T(8,128)(2,1)} copy(bf16[256,8,16,128]{3,1,2,0:T(8,128)(2,1)} %fusion.11) | data formatting | bytes 16777216
  89.9 8.9 %copy.23 = bf16[32,64,16,128]{3,1,0,2:T(8,128)(2,1)} copy(bf16[32,64,16,128]{3,2,1,0:T(8,128)(2,1)} %bitcast.29) | data formatting | bytes 16777216 | tf_op jit(solution)/shard_map/reshape | solution.py:179
  98.8 7.6 %all-to-all-start = ((bf16[16,32,64,128]{3,2,1,0:T(8,128)(2,1)}), bf16[16,32,64,128]{3,2,1,0:T(8,128)(2,1)}, u32[]{:S(2)}, u32[]{:S(2)}) async-start(bf16[16,32,64,128]{3,2,1,0:T(8,128)(2,1)} %bitcast.28), calls=%async_computation | async-start | bytes 16777216 | tf_op jit(solution)/shard_map/all_to_all | solution.py:181
  106.7 0.5 select_reduce_fusion
  107.2 0.3 fusion.71
  107.6 1.0 fusion.27
  108.7 0.8 dynamic_slice.11
  110.0 0.5 fusion.14
  110.7 1.3 pad_maximum_fusion.1
  112.0 0.8 add_select_fusion.1.e_ref
  112.8 1.2 subtract_convert_fusion.1
  114.0 2.4 pad_maximum_fusion.w_ref
  116.4 174.2 %all-to-all-done.r_ref = bf16[16,32,64,128]{3,2,1,0:T(8,128)(2,1)} async-done(((bf16[16,32,64,128]{3,2,1,0:T(8,128)(2,1)}), bf16[16,32,64,128]{3,2,1,0:T(8,128)(2,1)}, u32[]{:S(2)}, u32[]{:S(2)}) %all-to-all-start) | async-done | bytes 8388640 | tf_op jit(solution)/shard_map/all_to_all | solution.py:181
  290.6 30.5 %shard_map.64 = f32[1024,1024]{1,0:T(8,128)} custom-call(bf16[16,32,64,128]{3,2,1,0:T(8,128)(2,1)} %all-to-all-done.r_ref, f32[1024,128]{1,0:T(8,128)} %get-tuple-element.57.ga_ref, f32[1024,128]{1,0:T(8,128)} %get-tuple-element.58.gb_ref, bf16[1024,2048]{1,0:T(8,128)(2,1)} %pad_maximum_fusion.w_ref, s32[64,1024]{1,0:T(8,128)} %add_select_fusion.1.e_ref), custom_call_target="tpu_custom_call" | custom-call | tf_op jit(solution)/shard_map/pallas_call | solution.py:136
  321.1 2.5 convert_element_type.97
  323.6 50.6 %all_to_all.10 = bf16[32,32,1024]{2,1,0:T(8,128)(2,1)S(1)} all-to-all(bf16[32,32,1024]{2,1,0:T(8,128)(2,1)S(1)} %bitcast.30), channel_id=1, replica_groups=mesh['grp'=4,'mem'=4,'pair'=2] {'pair','grp','mem'}, dimensions={0} | all-to-all | bytes 4194304 | tf_op jit(solution)/shard_map/all_to_all | solution.py:212
  374.2 0.4 convert_reduce_fusion
  374.5 1.0 reshape.376
  (33 shorter events, 1.8 us)
Async XLA Ops:
  0.0 106.4 %copy-start = (f32[64,2,256]{2,1,0:T(2,128)S(1)}, f32[64,2,256]{2,1,0:T(2,128)}, u32[]{:S(2)}) copy-start(f32[64,2,256]{2,1,0:T(2,128)} %param.7) | copy-start | bytes 393220
  98.8 7.9 %copy-start.3 = (s32[1024]{0:T(1024)S(1)}, s32[1024]{0:T(1024)}, u32[]{:S(2)}) copy-start(s32[1024]{0:T(1024)} %param.9) | copy-start | bytes 12292
  98.8 10.6 %copy-start.2 = (s32[32,1024]{1,0:T(8,128)S(1)}, s32[32,1024]{1,0:T(8,128)}, u32[]{:S(2)}) copy-start(s32[32,1024]{1,0:T(8,128)} %param.10) | copy-start | bytes 393220
  98.8 11.2 %copy-start.1 = (s32[1024,2]{0,1:T(2,128)S(1)}, s32[1024,2]{0,1:T(2,128)}, u32[]{:S(2)}) copy-start(s32[1024,2]{0,1:T(2,128)} %param.8) | copy-start | bytes 24580
  98.8 191.8 %all-to-all-start = ((bf16[16,32,64,128]{3,2,1,0:T(8,128)(2,1)}), bf16[16,32,64,128]{3,2,1,0:T(8,128)(2,1)}, u32[]{:S(2)}, u32[]{:S(2)}) async-start(bf16[16,32,64,128]{3,2,1,0:T(8,128)(2,1)} %bitcast.28), calls=%async_computation | async-start | bytes 16777216 | tf_op jit(solution)/shard_map/all_to_all | solution.py:181

commit v2 on v1

v2 whole, which is shorter than its diff:
```python
import functools
import math

import jax
import jax.numpy as jnp
from jax import lax
from jax.experimental import pallas as pl
from jax.experimental.pallas import tpu as pltpu
from jax.sharding import PartitionSpec as P

NFFT = 2048
CHANS = 1024
TAPS = 4
CYL = 4
NS = 256
FEEDS = 1024
BEAMS = 1024
TIMES = 32
TRIALS = 32
PEERS = ("grp", "mem")
LANES = 128


def pfb_window(tap_count, length):
    offsets = jnp.arange(tap_count * length, dtype=jnp.float32) + 0.5
    shaped = jnp.sinc((offsets - tap_count * length / 2.0) / length)
    taper_term = 0.5 - 0.5 * jnp.cos(offsets * (2.0 * math.pi / (tap_count * length)))
    return (shaped * taper_term).reshape(tap_count, length)


def turn(index, length):
    angles = (index % length).astype(jnp.float32) * (2.0 * math.pi / length)
    return lax.optimization_barrier((jnp.cos(angles), jnp.sin(angles)))


def times(a, b):
    return (a[0] * b[0] - a[1] * b[1], a[0] * b[1] + a[1] * b[0])


def channel_table(chan_of, quarter):
    chan = chan_of[None, :]
    high = turn(jnp.arange(16, dtype=jnp.int32)[:, None] * 128 * chan, NFFT)
    mid = turn(jnp.arange(16, dtype=jnp.int32)[:, None] * 8 * chan, NFFT)
    low = turn(jnp.arange(8, dtype=jnp.int32)[:, None] * chan + quarter[None, :] * (NFFT // 4), NFFT)
    upper = times([p[:, None, :] for p in high], [p[None, :, :] for p in mid])
    upper = lax.optimization_barrier(tuple(p.reshape(NFFT // 8, 1, -1) for p in upper))
    table = upper[0] * low[0][None] - upper[1] * low[1][None]
    return table.astype(jnp.bfloat16).reshape(NFFT, -1)


def beam_weights(cylinder_map):
    slots = jnp.arange(FEEDS, dtype=jnp.int32)
    hit = cylinder_map[:, None] == slots[None, :]
    slot_of = jnp.sum(jnp.where(hit, slots[:, None], 0), axis=0)
    cyl, pos = slot_of // NS, slot_of % NS
    e = jnp.arange(CYL, dtype=jnp.int32).reshape(CYL, 1, 1)
    hh = jnp.arange(16, dtype=jnp.int32).reshape(1, 16, 1)
    upper = turn(16 * pos * hh + (NS // CYL) * e * cyl, NS)
    a = jnp.arange(2, dtype=jnp.int32).reshape(2, 1, 1)
    hl = jnp.arange(8, dtype=jnp.int32).reshape(1, 8, 1)
    lower = turn(pos * (2 * hl + a), NS)
    real, imag = times(
        [p[None, :, :, None, :] for p in upper], [p[:, None, None, :, :] for p in lower]
    )
    return jnp.concatenate(
        [p.astype(jnp.bfloat16).reshape(BEAMS, FEEDS) for p in (real, imag)], axis=1
    )


CHUNKS = (4, 12, 12, 4)


def dft_kernel(frames, feeds, window_ref, volt_ref, table_ref, out_ref, framed_ref):
    @pl.when(pl.program_id(0) == 0)
    def _():
        for t in range(frames):
            total = volt_ref[:, t * NFFT : (t + 1) * NFFT].astype(jnp.float32) * window_ref[0:1, :]
            for j in range(1, TAPS):
                tap = volt_ref[:, (t + j) * NFFT : (t + j + 1) * NFFT].astype(jnp.float32)
                total = total + tap * window_ref[j : j + 1, :]
            framed_ref[t * feeds : (t + 1) * feeds, :] = total.astype(jnp.bfloat16)

    part = jnp.dot(framed_ref[...], table_ref[...], preferred_element_type=jnp.float32)
    part = (part * (1.0 / math.sqrt(NFFT))).astype(jnp.bfloat16)
    for i in range(out_ref.shape[0]):
        out_ref[i] = part[:, i * LANES : (i + 1) * LANES].reshape(frames, feeds, LANES)


def dft_stage(voltages, window, table, start, frames, peers):
    feeds = voltages.shape[0]
    length = (frames + TAPS - 1) * NFFT
    volt = lax.slice_in_dim(voltages, start * NFFT, start * NFFT + length, axis=2)
    volt = volt.reshape(feeds, length)
    width = table.shape[1] // peers
    if width != LANES:
        view = volt.reshape(feeds, frames + TAPS - 1, NFFT).astype(jnp.float32)
        framed = view[:, 0:frames] * window[0]
        for j in range(1, TAPS):
            framed = framed + view[:, j : j + frames] * window[j]
        rows = jnp.swapaxes(framed.astype(jnp.bfloat16), 0, 1).reshape(frames * feeds, NFFT)
        part = jnp.dot(rows, table, preferred_element_type=jnp.float32) * (1.0 / math.sqrt(NFFT))
        part = part.astype(jnp.bfloat16).reshape(frames, feeds, peers, width)
        return jnp.moveaxis(part, 2, 0)
    step = 4
    return pl.pallas_call(
        functools.partial(dft_kernel, frames, feeds),
        grid=(peers // step,),
        out_shape=jax.ShapeDtypeStruct((peers, frames, feeds, width), jnp.bfloat16),
        in_specs=[
            pl.BlockSpec((TAPS, NFFT), lambda i: (0, 0)),
            pl.BlockSpec((feeds, length), lambda i: (0, 0)),
            pl.BlockSpec((NFFT, step * width), lambda i: (0, i)),
        ],
        out_specs=pl.BlockSpec((step, frames, feeds, width), lambda i: (i, 0, 0, 0)),
        scratch_shapes=[pltpu.VMEM((frames * feeds, NFFT), jnp.bfloat16)],
        compiler_params=pltpu.CompilerParams(
            dimension_semantics=("arbitrary",), vmem_limit_bytes=56 * 1024 * 1024
        ),
    )(window, volt, table)


HIT = (TIMES - 1) / (TIMES * TIMES)
MISS = -1.0 / (TIMES * TIMES)


def beam_kernel(start, frames, chans, r_ref, ga_ref, gb_ref, w_ref, e_ref, *rest):
    acc_ref = rest[0] if len(rest) == 5 else None
    out_ref, x_ref, t_ref, p_ref = rest[-4:]
    width = 2 * chans
    lane = lax.broadcasted_iota(jnp.int32, (FEEDS, width), 1)
    sign = jnp.where(lane < chans, 1.0, -1.0)
    low = lax.broadcasted_iota(jnp.int32, (BEAMS, width), 1) < chans

    def calibrate(i, carry):
        volt = r_ref[:, i].reshape(FEEDS, width).astype(jnp.float32)
        cal = volt * ga_ref[...] + pltpu.roll(volt, chans, 1) * gb_ref[...]
        turned = pltpu.roll(cal, chans, 1) * sign
        cols = pl.ds(pl.multiple_of(i * width, width), width)
        x_ref[0:FEEDS, cols] = cal.astype(jnp.bfloat16)
        x_ref[FEEDS : 2 * FEEDS, cols] = turned.astype(jnp.bfloat16)
        hit = e_ref[...] == start + i
        rows = pl.ds(pl.multiple_of(i * chans, chans), chans)
        t_ref[rows, :] = jnp.where(hit, HIT, MISS).astype(jnp.bfloat16)
        return carry

    def form(i, carry):
        cols = pl.ds(pl.multiple_of(i * 2 * width, 2 * width), 2 * width)
        beams = jnp.dot(w_ref[...], x_ref[:, cols], preferred_element_type=jnp.float32)
        squares = beams * beams
        one, two = squares[:, :width], squares[:, width:]
        first = one + pltpu.roll(one, chans, 1)
        second = two + pltpu.roll(two, chans, 1)
        power = jnp.where(low, first, second) * (1.0 / FEEDS)
        p_ref[:, pl.ds(pl.multiple_of(i * width, width), width)] = power.astype(jnp.bfloat16)
        return carry

    lax.fori_loop(0, frames, calibrate, 0)
    lax.fori_loop(0, frames // 2, form, 0)
    part = jnp.dot(p_ref[...], t_ref[...], preferred_element_type=jnp.float32)
    if acc_ref is not None:
        part = part + acc_ref[...]
    out_ref[...] = part.astype(out_ref.dtype)


def beam_stage(received, gains, weights, shift, start, acc):
    _, frames, _, width = received.shape
    chans = width // 2
    last = start + frames == TIMES
    held = jnp.bfloat16 if last else jnp.float32
    if width != LANES:
        volt = jnp.moveaxis(received, 1, 0).reshape(frames, FEEDS, 2, chans).astype(jnp.float32)
        ga, gb = (g.reshape(FEEDS, 2, chans) for g in gains)
        cal = (volt * ga + volt[:, :, ::-1] * gb).astype(jnp.bfloat16)
        turned = jnp.stack([cal[:, :, 1], -cal[:, :, 0]], axis=2)
        both = jnp.concatenate([cal, turned], axis=1)
        beams = jnp.einsum("bf,tfrc->btrc", weights, both, preferred_element_type=jnp.float32)
        power = jnp.sum(beams * beams, axis=2) * (1.0 / FEEDS)
        power = power.astype(jnp.bfloat16).reshape(BEAMS, frames * chans)
        frame = start + jnp.arange(frames, dtype=jnp.int32)[:, None, None]
        spread = jnp.where(shift[None] == frame, HIT, MISS).astype(jnp.bfloat16)
        spread = spread.reshape(frames * chans, -1)
        part = jnp.dot(power, spread, preferred_element_type=jnp.float32)
        return (part if acc is None else part + acc).astype(held)
    series = TRIALS * TIMES
    operands = (received, *gains, weights, shift) + (() if acc is None else (acc,))
    return pl.pallas_call(
        functools.partial(beam_kernel, start, frames, chans),
        out_shape=jax.ShapeDtypeStruct((BEAMS, series), held),
        in_specs=[pl.BlockSpec(memory_space=pltpu.VMEM)] * len(operands),
        out_specs=pl.BlockSpec(memory_space=pltpu.VMEM),
        scratch_shapes=[
            pltpu.VMEM((2 * FEEDS, frames * width), jnp.bfloat16),
            pltpu.VMEM((frames * chans, series), jnp.bfloat16),
            pltpu.VMEM((BEAMS, frames * chans), jnp.bfloat16),
        ],
        compiler_params=pltpu.CompilerParams(vmem_limit_bytes=56 * 1024 * 1024),
    )(*operands)


def local(voltages, gain_table, gain_index, cylinder_map, delays, chan_map):
    feeds = voltages.shape[0]
    grp_count, mem_count = lax.axis_size("grp"), lax.axis_size("mem")
    peers = grp_count * mem_count
    chans = CHANS // peers
    grp, mem = lax.axis_index("grp"), lax.axis_index("mem")

    window = pfb_window(TAPS, NFFT)
    peer = jnp.arange(peers, dtype=jnp.int32)
    base = peer % mem_count * (CHANS // mem_count) + peer // mem_count * chans
    chan_of = base[:, None, None] + jnp.arange(chans, dtype=jnp.int32)[None, None, :]
    quarter = jnp.arange(2, dtype=jnp.int32)[None, :, None]
    chan_of, quarter = (
        jnp.broadcast_to(v, (peers, 2, chans)).reshape(-1) for v in (chan_of, quarter)
    )
    table = channel_table(chan_of, quarter)

    table = lax.optimization_barrier(table)
    starts = [sum(CHUNKS[:i]) for i in range(len(CHUNKS))]

    def exchange(spectra):
        return lax.all_to_all(spectra, PEERS, split_axis=0, concat_axis=0, tiled=True)

    spectra = [
        dft_stage(voltages, window, table, start, frames, peers)
        for start, frames in zip(starts, CHUNKS)
    ]
    received = [exchange(block) for block in spectra[:-1]]

    pairs = lax.axis_size("pair")
    cores = 2 if grp_count % 2 == 0 else 1
    owned = BEAMS // (pairs * peers)
    weights = beam_weights(cylinder_map)
    weights = weights.reshape(pairs, grp_count // cores, cores, mem_count * owned, 2 * FEEDS)
    weights = jnp.moveaxis(weights, 2, 0).reshape(BEAMS, 2 * FEEDS)
    gain_here = lax.dynamic_slice_in_dim(gain_table, grp * chans, chans, 2)
    gain_rows = gain_index[:, lax.axis_index("pair")]
    pick = gain_rows[:, None] == jnp.arange(gain_table.shape[0], dtype=jnp.int32)[None, :]
    gain_values = jnp.dot(
        pick.astype(jnp.float32),
        gain_here.reshape(gain_table.shape[0], 2 * chans),
        precision=lax.Precision.HIGHEST,
    )
    gain_real, gain_imag = gain_values[:, :chans], gain_values[:, chans:]
    gains = (
        jnp.concatenate([gain_real, gain_real], axis=1),
        jnp.concatenate([-gain_imag, gain_imag], axis=1),
    )

    first = mem * (CHANS // mem_count) + grp * chans
    freq = lax.dynamic_slice_in_dim(chan_map, first, chans, 0)
    column = jnp.arange(CHANS, dtype=jnp.int32)[:, None] == freq[None, :]
    delay = jnp.dot(
        delays.astype(jnp.bfloat16), column.astype(jnp.bfloat16), preferred_element_type=jnp.float32
    ).astype(jnp.int32)
    frame = jnp.arange(TIMES, dtype=jnp.int32)[None, None, :]
    shift = ((frame - delay.T[:, :, None]) % TIMES).reshape(chans, TRIALS * TIMES)

    part = None
    for i, start in enumerate(starts):
        if i == len(starts) - 1:
            last, part = lax.optimization_barrier((spectra[-1], held))
            received.append(exchange(last))
            part = beam_stage(received[i - 1], gains, weights, shift, starts[i - 1], part)
        if i == len(starts) - 2:
            held = part
            continue
        part = beam_stage(received[i], gains, weights, shift, start, part)

    series = TRIALS * TIMES
    groups = [[x * cores + c for c in range(cores)] for x in range(grp_count // cores)]
    part = part.reshape(cores, BEAMS // cores, series)
    part = lax.all_to_all(
        part, "grp", split_axis=0, concat_axis=0, axis_index_groups=groups, tiled=True
    )
    part = jnp.sum(part.astype(jnp.float32), axis=0).astype(jnp.bfloat16)
    part = part.reshape(pairs * peers // cores, owned, series)
    groups = [
        [
            (p * grp_count + x * cores + c) * mem_count + m
            for p in range(pairs)
            for x in range(grp_count // cores)
            for m in range(mem_count)
        ]
        for c in range(cores)
    ]
    part = lax.all_to_all(
        part, ("pair",) + PEERS, split_axis=0, concat_axis=0, axis_index_groups=groups, tiled=True
    )
    series = jnp.sum(part.astype(jnp.float32), axis=0)
    return series.reshape(1, owned, TRIALS, TIMES)


def solution(mesh):
    return jax.shard_map(
        local,
        mesh=mesh,
        in_specs=(P(PEERS, "pair", None), P(None, None, "mem"), P(), P(), P(), P()),
        out_specs=P("pair", PEERS, None, None),
        check_vma=False,
    )
```

time: 377 us -> 290 us (0.77)
  waiting for transfers between devices: 174 us -> 92.1 us
  Pallas kernels: 30.5 us -> 102 us
  local copies, waits for them, and re-layouts: 45.1 us -> 17.4 us
  other arithmetic: 44.5 us -> 17.1 us
  matrix products: 22.8 us -> 1.58 us
  starting transfers between devices: 7.58 us -> 19.7 us
  blocking collectives: 50.6 us -> 38.6 us
    all_to_all x1 -> x4, waiting for transfers between devices: 174 us -> 92.1 us  [exchange(): lax.all_to_all(spectra, PEERS, split_axis=0, concat_axis=0, tiled=True)]
    pallas_call x1 -> x8, Pallas kernels: 30.5 us -> 102 us  [the longest x4 60.4 us: beam_stage(): pl.pallas_call(functools.partial(beam_kernel, start, frames, chans), out_...]
    transpose x1 -> x0, other arithmetic: 31.6 us -> none  [local(): rows = jnp.swapaxes(framed, 0, 1).reshape(TIMES * feeds, NFFT)]
    dot_general x1 -> x0, matrix products: 22.1 us -> none  [local(): jnp.dot(rows, table, preferred_element_type=jnp.float32)]
    convert_element_type x1 -> x0, local copies, waits for them, and re-layouts: 12.8 us -> none  [frame_signal(): volt_rows.reshape(leading, TIMES + TAPS - 1, NFFT).astype(jnp.float32)]
    all_to_all x1 -> x4, starting transfers between devices: 7.58 us -> 19.7 us  [exchange(): lax.all_to_all(spectra, PEERS, split_axis=0, concat_axis=0, tiled=True)]
    all_to_all x1 -> x2, blocking collectives: 50.6 us -> 38.6 us  [the longest x1 31.9 us: local(): lax.all_to_all(part, ('pair',) + PEERS, split_axis=0, concat_axis=0, axis...]
    transpose x1 -> x0, local copies, waits for them, and re-layouts: 11.2 us -> none  [local(): rows = jnp.swapaxes(framed, 0, 1).reshape(TIMES * feeds, NFFT)]
  transfers between devices with their start and end apart: 1 -> 4, of which waited for: 1 -> 4; matrix products, arithmetic and copies ran while one was open for 3% -> 7% of each run, Pallas kernels for 0% -> 29%
where the time goes in v2:
time: 290 us; the launch traced here: 289 us
  Pallas kernels  102 us (35%)
  waiting for transfers between devices  92.1 us (32%)
  blocking collectives  38.6 us (13%)
  starting transfers between devices  19.7 us (7%)
  local copies, waits for them, and re-layouts  17.4 us (6%)
  other arithmetic  17.1 us (6%)
    all_to_all x4, waiting for transfers between devices, exchange(): lax.all_to_all(spectra, PEERS, split_axis=0, concat_axis=0, tiled=True)  92.1 us
    pallas_call x4, Pallas kernels, beam_stage(): pl.pallas_call(functools.partial(beam_kernel, start, frames, chans), out_...  60.4 us
    pallas_call x4, Pallas kernels, dft_stage(): pl.pallas_call(functools.partial(dft_kernel, frames, feeds), grid=(peers...  41.9 us
    all_to_all x1, blocking collectives, local(): lax.all_to_all(part, ('pair',) + PEERS, split_axis=0, concat_axis=0, axis...  31.9 us
    all_to_all x4, starting transfers between devices, exchange(): lax.all_to_all(spectra, PEERS, split_axis=0, concat_axis=0, tiled=True)  19.7 us
    reshape x2, local copies, waits for them, and re-layouts, dft_stage(): volt = volt.reshape(feeds, length)  9.7 us
    all_to_all x1, blocking collectives, local(): lax.all_to_all(part, 'grp', split_axis=0, concat_axis=0, axis_index_group...  6.75 us
  transfers between devices with their start and end apart: 4, of which 4 were waited for; matrix products, arithmetic and copies ran while one was open for 7% of the time, Pallas kernels for 29%

profile of v2, /device:TPU:0, one launch (start us, length us, event | category | flops | bytes accessed | tf_op | source)
XLA Modules:
  0.0 289.0 jit_solution(1537775287754301401)
XLA Ops:
  3.2 4.3 %slice_bitcast_fusion.2 = (bf16[64,14336]{1,0:T(8,128)(2,1)}, bf16[64,14336]{1,0:T(8,128)(2,1)}) fusion(bf16[64,1,71680]{2,0,1:T(8,128)(2,1)} %param.6), kind=kLoop, calls=%fused_computation.12 | loop fusion | bytes 7340032 | tf_op jit(solution)/shard_map/reshape | solution.py:93
  7.4 4.8 %fusion.table_ref = bf16[2048,2048]{1,0:T(8,128)(2,1)} fusion(f32[8,2048]{1,0:T(8,128)S(1)} %get-tuple-element.26, f32[256,2048]{1,0:T(8,128)S(1)} %bitcast.32, f32[8,2048]{1,0:T(8,128)S(1)} %get-tuple-element.24, f32[256,2048]{1,0:T(8,128)S(1)} %bitcast.33), kind=kLoop, calls=%fused_computation.1 | loop fusion | flops 16777216 | bytes 12713984 | tf_op jit(solution)/shard_map/convert_element_type | solution.py:48
  12.2 7.6 %shard_map.66 = bf16[16,4,64,128]{3,2,1,0:T(8,128)(2,1)} custom-call(f32[4,2048]{1,0:T(4,128)} %fusion.34.window_ref, bf16[64,14336]{1,0:T(8,128)(2,1)} %get-tuple-element.35.volt_ref, bf16[2048,2048]{1,0:T(8,128)(2,1)} %fusion.table_ref), custom_call_target="tpu_custom_call" | custom-call | tf_op jit(solution)/shard_map/pallas_call | solution.py:105
  19.9 7.4 %all-to-all-start.1 = ((bf16[16,4,64,128]{3,2,1,0:T(8,128)(2,1)}), bf16[16,4,64,128]{3,2,1,0:T(8,128)(2,1)S(1)}, u32[]{:S(2)}, u32[]{:S(2)}) async-start(bf16[16,4,64,128]{3,2,1,0:T(8,128)(2,1)} %shard_map.66), calls=%async_computation.1 | async-start | bytes 2097152 | tf_op jit(solution)/shard_map/all_to_all | solution.py:221
  27.3 5.4 %slice_bitcast_fusion = (bf16[64,30720]{1,0:T(8,128)(2,1)}, bf16[64,30720]{1,0:T(8,128)(2,1)}) fusion(bf16[64,1,71680]{2,0,1:T(8,128)(2,1)} %param.6), kind=kLoop, calls=%fused_computation.7 | loop fusion | bytes 15728640 | tf_op jit(solution)/shard_map/reshape | solution.py:93
  32.7 13.3 %shard_map.65 = bf16[16,12,64,128]{3,2,1,0:T(8,128)(2,1)} custom-call(f32[4,2048]{1,0:T(4,128)} %fusion.34.window_ref, bf16[64,30720]{1,0:T(8,128)(2,1)} %get-tuple-element.34.volt_ref, bf16[2048,2048]{1,0:T(8,128)(2,1)} %fusion.table_ref), custom_call_target="tpu_custom_call" | custom-call | tf_op jit(solution)/shard_map/pallas_call | solution.py:105
  46.0 8.1 %all-to-all-done.1.r_ref = bf16[16,4,64,128]{3,2,1,0:T(8,128)(2,1)S(1)} async-done(((bf16[16,4,64,128]{3,2,1,0:T(8,128)(2,1)}), bf16[16,4,64,128]{3,2,1,0:T(8,128)(2,1)S(1)}, u32[]{:S(2)}, u32[]{:S(2)}) %all-to-all-start.1) | async-done | bytes 1048608 | tf_op jit(solution)/shard_map/all_to_all | solution.py:221
  55.1 3.9 %all-to-all-start = ((bf16[16,12,64,128]{3,2,1,0:T(8,128)(2,1)}), bf16[16,12,64,128]{3,2,1,0:T(8,128)(2,1)S(1)}, u32[]{:S(2)}, u32[]{:S(2)}) async-start(bf16[16,12,64,128]{3,2,1,0:T(8,128)(2,1)} %shard_map.65), calls=%async_computation | async-start | bytes 6291456 | tf_op jit(solution)/shard_map/all_to_all | solution.py:221
  59.1 13.3 %shard_map.69 = bf16[16,12,64,128]{3,2,1,0:T(8,128)(2,1)} custom-call(f32[4,2048]{1,0:T(4,128)} %fusion.34.window_ref, bf16[64,30720]{1,0:T(8,128)(2,1)} %get-tuple-element.33.volt_ref, bf16[2048,2048]{1,0:T(8,128)(2,1)} %fusion.table_ref), custom_call_target="tpu_custom_call" | custom-call | tf_op jit(solution)/shard_map/pallas_call | solution.py:105
  72.4 58.3 %all-to-all-done.r_ref = bf16[16,12,64,128]{3,2,1,0:T(8,128)(2,1)S(1)} async-done(((bf16[16,12,64,128]{3,2,1,0:T(8,128)(2,1)}), bf16[16,12,64,128]{3,2,1,0:T(8,128)(2,1)S(1)}, u32[]{:S(2)}, u32[]{:S(2)}) %all-to-all-start) | async-done | bytes 3145760 | tf_op jit(solution)/shard_map/all_to_all | solution.py:221
  130.7 4.5 %all-to-all-start.3 = ((bf16[16,12,64,128]{3,2,1,0:T(8,128)(2,1)}), bf16[16,12,64,128]{3,2,1,0:T(8,128)(2,1)}, u32[]{:S(2)}, u32[]{:S(2)}) async-start(bf16[16,12,64,128]{3,2,1,0:T(8,128)(2,1)} %shard_map.69), calls=%async_computation.3 | async-start | bytes 6291456 | tf_op jit(solution)/shard_map/all_to_all | solution.py:221
  137.1 1.7 fusion.14
  142.8 7.7 %shard_map.64 = bf16[16,4,64,128]{3,2,1,0:T(8,128)(2,1)} custom-call(f32[4,2048]{1,0:T(4,128)} %fusion.34.window_ref, bf16[64,14336]{1,0:T(8,128)(2,1)} %get-tuple-element.36.volt_ref, bf16[2048,2048]{1,0:T(8,128)(2,1)} %fusion.table_ref), custom_call_target="tpu_custom_call" | custom-call | tf_op jit(solution)/shard_map/pallas_call | solution.py:105
  151.2 1.3 pad_maximum_fusion.1
  155.3 2.4 pad_maximum_fusion
  157.7 9.5 %shard_map.67.rest_0_ = f32[1024,1024]{1,0:T(8,128)} custom-call(bf16[16,4,64,128]{3,2,1,0:T(8,128)(2,1)} %copy-done.4, f32[1024,128]{1,0:T(8,128)} %get-tuple-element.61.ga_ref, f32[1024,128]{1,0:T(8,128)} %get-tuple-element.62.gb_ref, bf16[1024,2048]{1,0:T(8,128)(2,1)} %bitcast.28, s32[64,1024]{1,0:T(8,128)} %add_select_fusion.1.e_ref), custom_call_target="tpu_custom_call" | custom-call | tf_op jit(solution)/shard_map/pallas_call | solution.py:186
  167.2 20.3 %shard_map.68.rest_0_ = f32[1024,1024]{1,0:T(8,128)} custom-call(bf16[16,12,64,128]{3,2,1,0:T(8,128)(2,1)} %copy-done.2, f32[1024,128]{1,0:T(8,128)} %get-tuple-element.61.ga_ref, f32[1024,128]{1,0:T(8,128)} %get-tuple-element.62.gb_ref, bf16[1024,2048]{1,0:T(8,128)(2,1)} %bitcast.29, s32[64,1024]{1,0:T(8,128)} %add_select_fusion.1.e_ref, ...), custom_call_target="tpu_custom_call" | custom-call | tf_op jit(solution)/shard_map/pallas_call | solution.py:186
  187.5 19.4 %all-to-all-done.3.r_ref = bf16[16,12,64,128]{3,2,1,0:T(8,128)(2,1)} async-done(((bf16[16,12,64,128]{3,2,1,0:T(8,128)(2,1)}), bf16[16,12,64,128]{3,2,1,0:T(8,128)(2,1)}, u32[]{:S(2)}, u32[]{:S(2)}) %all-to-all-start.3) | async-done | bytes 3145760 | tf_op jit(solution)/shard_map/all_to_all | solution.py:221
  207.0 3.9 %all-to-all-start.2 = ((bf16[16,4,64,128]{3,2,1,0:T(8,128)(2,1)}), bf16[16,4,64,128]{3,2,1,0:T(8,128)(2,1)S(1)}, u32[]{:S(2)}, u32[]{:S(2)}) async-start(bf16[16,4,64,128]{3,2,1,0:T(8,128)(2,1)} %shard_map.64), calls=%async_computation.2 | async-start | bytes 2097152 | tf_op jit(solution)/shard_map/all_to_all | solution.py:221
  210.9 20.4 %shard_map.70.rest_0_ = f32[1024,1024]{1,0:T(8,128)} custom-call(bf16[16,12,64,128]{3,2,1,0:T(8,128)(2,1)} %all-to-all-done.3.r_ref, f32[1024,128]{1,0:T(8,128)} %get-tuple-element.61.ga_ref, f32[1024,128]{1,0:T(8,128)} %get-tuple-element.62.gb_ref, bf16[1024,2048]{1,0:T(8,128)(2,1)} %bitcast.30, s32[64,1024]{1,0:T(8,128)} %add_select_fusion.1.e_ref, ...), custom_call_target="tpu_custom_call" | custom-call | tf_op jit(solution)/shard_map/pallas_call | solution.py:186
  231.2 6.2 %all-to-all-done.2.r_ref = bf16[16,4,64,128]{3,2,1,0:T(8,128)(2,1)S(1)} async-done(((bf16[16,4,64,128]{3,2,1,0:T(8,128)(2,1)}), bf16[16,4,64,128]{3,2,1,0:T(8,128)(2,1)S(1)}, u32[]{:S(2)}, u32[]{:S(2)}) %all-to-all-start.2) | async-done | bytes 1048608 | tf_op jit(solution)/shard_map/all_to_all | solution.py:221
  238.4 10.2 %shard_map.71 = bf16[1024,1024]{1,0:T(8,128)(2,1)} custom-call(bf16[16,4,64,128]{3,2,1,0:T(8,128)(2,1)} %copy-done.3, f32[1024,128]{1,0:T(8,128)} %get-tuple-element.61.ga_ref, f32[1024,128]{1,0:T(8,128)} %get-tuple-element.62.gb_ref, bf16[1024,2048]{1,0:T(8,128)(2,1)} %bitcast.31, s32[64,1024]{1,0:T(8,128)} %add_select_fusion.1.e_ref, ...), custom_call_target="tpu_custom_call" | custom-call | tf_op jit(solution)/shard_map/pallas_call | solution.py:186
  248.6 6.7 %all_to_all.30 = bf16[2,512,1024]{2,1,0:T(8,128)(2,1)S(1)} all-to-all(bf16[2,512,1024]{2,1,0:T(8,128)(2,1)} %bitcast.36), channel_id=1, replica_groups={{0,8},{16,24},{1,9},{17,25},{2,10},{18,26},{3,11},{19,27},{4,12},{20,28..., dimensions={0} | all-to-all | bytes 4194304 | tf_op jit(solution)/shard_map/all_to_all | solution.py:272
  256.0 31.9 %all_to_all.31 = bf16[16,32,1024]{2,1,0:T(8,128)(2,1)S(1)} all-to-all(bf16[16,32,1024]{2,1,0:T(8,128)(2,1)S(1)} %bitcast.37), channel_id=1, replica_groups={{0,2,4,6,16,18,20,22,1,3,5,7,17,19,21,23},{8,10,12,14,24,26,28,30,9,11,..., dimensions={0} | all-to-all | bytes 2097152 | tf_op jit(solution)/shard_map/all_to_all | solution.py:286
  (56 shorter events, 16.1 us)
Async XLA Ops:
  0.0 135.2 %copy-start = (f32[64,2,256]{2,1,0:T(2,128)S(1)}, f32[64,2,256]{2,1,0:T(2,128)}, u32[]{:S(2)}) copy-start(f32[64,2,256]{2,1,0:T(2,128)} %param.7) | copy-start | bytes 393220
  19.9 34.2 %all-to-all-start.1 = ((bf16[16,4,64,128]{3,2,1,0:T(8,128)(2,1)}), bf16[16,4,64,128]{3,2,1,0:T(8,128)(2,1)S(1)}, u32[]{:S(2)}, u32[]{:S(2)}) async-start(bf16[16,4,64,128]{3,2,1,0:T(8,128)(2,1)} %shard_map.66), calls=%async_computation.1 | async-start | bytes 2097152 | tf_op jit(solution)/shard_map/all_to_all | solution.py:221
  54.1 1.0 copy-start.4
  55.1 75.5 %all-to-all-start = ((bf16[16,12,64,128]{3,2,1,0:T(8,128)(2,1)}), bf16[16,12,64,128]{3,2,1,0:T(8,128)(2,1)S(1)}, u32[]{:S(2)}, u32[]{:S(2)}) async-start(bf16[16,12,64,128]{3,2,1,0:T(8,128)(2,1)} %shard_map.65), calls=%async_computation | async-start | bytes 6291456 | tf_op jit(solution)/shard_map/all_to_all | solution.py:221
  72.4 63.7 %copy-start.8 = (s32[1024]{0:T(1024)S(1)}, s32[1024]{0:T(1024)}, u32[]{:S(2)}) copy-start(s32[1024]{0:T(1024)} %param.9) | copy-start | bytes 12292
  130.7 10.9 %copy-start.2 = (bf16[16,12,64,128]{3,2,1,0:T(8,128)(2,1)}, bf16[16,12,64,128]{3,2,1,0:T(8,128)(2,1)S(1)}, u32[]{:S(2)}) copy-start(bf16[16,12,64,128]{3,2,1,0:T(8,128)(2,1)S(1)} %all-to-all-done.r_ref) | copy-start | bytes 9437188
  130.7 76.3 %all-to-all-start.3 = ((bf16[16,12,64,128]{3,2,1,0:T(8,128)(2,1)}), bf16[16,12,64,128]{3,2,1,0:T(8,128)(2,1)}, u32[]{:S(2)}, u32[]{:S(2)}) async-start(bf16[16,12,64,128]{3,2,1,0:T(8,128)(2,1)} %shard_map.69), calls=%async_computation.3 | async-start | bytes 6291456 | tf_op jit(solution)/shard_map/all_to_all | solution.py:221
  142.8 7.7 %copy-start.7 = (s32[1024,2]{0,1:T(2,128)S(1)}, s32[1024,2]{0,1:T(2,128)}, u32[]{:S(2)}) copy-start(s32[1024,2]{0,1:T(2,128)} %param.8) | copy-start | bytes 24580
  142.8 7.7 %copy-start.6 = (f32[64,128]{1,0:T(8,128)S(1)}, f32[64,128]{1,0:T(8,128)}, u32[]{:S(2)}) copy-start(f32[64,128]{1,0:T(8,128)} %reshape.372) | copy-start | bytes 98308
  151.0 2.6 copy-start.5
  207.0 30.5 %all-to-all-start.2 = ((bf16[16,4,64,128]{3,2,1,0:T(8,128)(2,1)}), bf16[16,4,64,128]{3,2,1,0:T(8,128)(2,1)S(1)}, u32[]{:S(2)}, u32[]{:S(2)}) async-start(bf16[16,4,64,128]{3,2,1,0:T(8,128)(2,1)} %shard_map.64), calls=%async_computation.2 | async-start | bytes 2097152 | tf_op jit(solution)/shard_map/all_to_all | solution.py:221
  237.5 1.0 copy-start.3
  248.6 40.3 %copy-start.1 = (f32[64,2,256]{2,1,0:T(2,128)S(1)}, f32[64,2,256]{2,1,0:T(2,128)}, u32[]{:S(2)}) copy-start(f32[64,2,256]{2,1,0:T(2,128)} %param.7) | copy-start | bytes 393220

commit v3 on v2

--- a/solution.py
+++ b/solution.py
@@ -67,7 +67,9 @@
     )
 
 
-CHUNKS = (4, 12, 12, 4)
+BEAM_VMEM = 40
+DFT_VMEM = 40
+CHUNKS = (8, 20, 4)
 
 
 def dft_kernel(frames, feeds, window_ref, volt_ref, table_ref, out_ref, framed_ref):
@@ -114,7 +116,7 @@
         out_specs=pl.BlockSpec((step, frames, feeds, width), lambda i: (i, 0, 0, 0)),
         scratch_shapes=[pltpu.VMEM((frames * feeds, NFFT), jnp.bfloat16)],
         compiler_params=pltpu.CompilerParams(
-            dimension_semantics=("arbitrary",), vmem_limit_bytes=56 * 1024 * 1024
+            dimension_semantics=("arbitrary",), vmem_limit_bytes=DFT_VMEM * 1024 * 1024
         ),
     )(window, volt, table)
 
@@ -124,38 +126,48 @@
 
 
 def beam_kernel(start, frames, chans, r_ref, ga_ref, gb_ref, w_ref, e_ref, *rest):
-    acc_ref = rest[0] if len(rest) == 5 else None
-    out_ref, x_ref, t_ref, p_ref = rest[-4:]
+    acc_ref = rest[0] if len(rest) == 6 else None
+    out_ref, even_ref, odd_ref, t_ref, p_ref = rest[-5:]
     width = 2 * chans
     lane = lax.broadcasted_iota(jnp.int32, (FEEDS, width), 1)
     sign = jnp.where(lane < chans, 1.0, -1.0)
     low = lax.broadcasted_iota(jnp.int32, (BEAMS, width), 1) < chans
 
-    def calibrate(i, carry):
-        volt = r_ref[:, i].reshape(FEEDS, width).astype(jnp.float32)
-        cal = volt * ga_ref[...] + pltpu.roll(volt, chans, 1) * gb_ref[...]
-        turned = pltpu.roll(cal, chans, 1) * sign
-        cols = pl.ds(pl.multiple_of(i * width, width), width)
-        x_ref[0:FEEDS, cols] = cal.astype(jnp.bfloat16)
-        x_ref[FEEDS : 2 * FEEDS, cols] = turned.astype(jnp.bfloat16)
-        hit = e_ref[...] == start + i
-        rows = pl.ds(pl.multiple_of(i * chans, chans), chans)
-        t_ref[rows, :] = jnp.where(hit, HIT, MISS).astype(jnp.bfloat16)
-        return carry
-
-    def form(i, carry):
-        cols = pl.ds(pl.multiple_of(i * 2 * width, 2 * width), 2 * width)
-        beams = jnp.dot(w_ref[...], x_ref[:, cols], preferred_element_type=jnp.float32)
+    def calibrate(pair, x_ref):
+        for u in range(2):
+            i = 2 * pair + u
+            volt = r_ref[:, i].reshape(FEEDS, width).astype(jnp.float32)
+            cal = volt * ga_ref[...] + pltpu.roll(volt, chans, 1) * gb_ref[...]
+            turned = pltpu.roll(cal, chans, 1) * sign
+            cols = slice(u * width, (u + 1) * width)
+            x_ref[0:FEEDS, cols] = cal.astype(jnp.bfloat16)
+            x_ref[FEEDS : 2 * FEEDS, cols] = turned.astype(jnp.bfloat16)
+            hit = e_ref[...] == start + i
+            rows = pl.ds(pl.multiple_of(i * chans, chans), chans)
+            t_ref[rows, :] = jnp.where(hit, HIT, MISS).astype(jnp.bfloat16)
+
+    def form(pair, x_ref):
+        beams = jnp.dot(w_ref[...], x_ref[...], preferred_element_type=jnp.float32)
         squares = beams * beams
         one, two = squares[:, :width], squares[:, width:]
         first = one + pltpu.roll(one, chans, 1)
         second = two + pltpu.roll(two, chans, 1)
         power = jnp.where(low, first, second) * (1.0 / FEEDS)
-        p_ref[:, pl.ds(pl.multiple_of(i * width, width), width)] = power.astype(jnp.bfloat16)
+        p_ref[:, pl.ds(pl.multiple_of(pair * width, width), width)] = power.astype(jnp.bfloat16)
+
+    pairs = frames // 2
+    calibrate(0, even_ref)
+
+    def body(k, carry):
+        form(2 * k, even_ref)
+        calibrate(2 * k + 1, odd_ref)
+        form(2 * k + 1, odd_ref)
+        calibrate(jnp.minimum(2 * k + 2, pairs - 1), even_ref)
         return carry
 
-    lax.fori_loop(0, frames, calibrate, 0)
-    lax.fori_loop(0, frames // 2, form, 0)
+    lax.fori_loop(0, pairs // 2, body, 0)
+    if pairs % 2:
+        form(pairs - 1, even_ref)
     part = jnp.dot(p_ref[...], t_ref[...], preferred_element_type=jnp.float32)
     if acc_ref is not None:
         part = part + acc_ref[...]
@@ -189,11 +201,12 @@
         in_specs=[pl.BlockSpec(memory_space=pltpu.VMEM)] * len(operands),
         out_specs=pl.BlockSpec(memory_space=pltpu.VMEM),
         scratch_shapes=[
-            pltpu.VMEM((2 * FEEDS, frames * width), jnp.bfloat16),
+            pltpu.VMEM((2 * FEEDS, 2 * width), jnp.bfloat16),
+            pltpu.VMEM((2 * FEEDS, 2 * width), jnp.bfloat16),
             pltpu.VMEM((frames * chans, series), jnp.bfloat16),
             pltpu.VMEM((BEAMS, frames * chans), jnp.bfloat16),
         ],
-        compiler_params=pltpu.CompilerParams(vmem_limit_bytes=56 * 1024 * 1024),
+        compiler_params=pltpu.CompilerParams(vmem_limit_bytes=BEAM_VMEM * 1024 * 1024),
     )(*operands)
 
 

time: 290 us -> 278 us (0.959)
  Pallas kernels: 102 us -> 61.5 us
  waiting for transfers between devices: 92.1 us -> 112 us
  local copies, waits for them, and re-layouts: 17.4 us -> 35.3 us
  other arithmetic: 17.1 us -> 10.8 us
  starting transfers between devices: 19.7 us -> 16.1 us
    pallas_call x4 -> x3, Pallas kernels: 60.4 us -> 31.8 us  [beam_stage(): pl.pallas_call(functools.partial(beam_kernel, start, frames, chans), out_...]
    unnamed x18 -> x38, local copies, waits for them, and re-layouts: 2.04 us -> 24.7 us
    all_to_all x4 -> x3, waiting for transfers between devices: 92.1 us -> 112 us  [exchange(): lax.all_to_all(spectra, PEERS, split_axis=0, concat_axis=0, tiled=True)]
    pallas_call x4 -> x3, Pallas kernels: 41.9 us -> 29.7 us  [dft_stage(): pl.pallas_call(functools.partial(dft_kernel, frames, feeds), grid=(peers...]
    all_to_all x4 -> x3, starting transfers between devices: 19.7 us -> 16.1 us  [exchange(): lax.all_to_all(spectra, PEERS, split_axis=0, concat_axis=0, tiled=True)]
    reshape x2 -> x3, local copies, waits for them, and re-layouts: 9.7 us -> 6.72 us  [dft_stage(): volt = volt.reshape(feeds, length)]
  transfers between devices with their start and end apart: 4 -> 3, of which waited for: 4 -> 2; matrix products, arithmetic and copies ran while one was open for 7% -> 5% of each run, Pallas kernels for 29% -> 18%
where the time goes in v3:
time: 278 us; the launch traced here: 277 us
  waiting for transfers between devices  112 us (40%)
  Pallas kernels  61.5 us (22%)
  blocking collectives  39.7 us (14%)
  local copies, waits for them, and re-layouts  35.3 us (13%)
  starting transfers between devices  16.1 us (6%)
  other arithmetic  10.8 us (4%)
    all_to_all x3, waiting for transfers between devices, exchange(): lax.all_to_all(spectra, PEERS, split_axis=0, concat_axis=0, tiled=True)  112 us
    all_to_all x1, blocking collectives, local(): lax.all_to_all(part, ('pair',) + PEERS, split_axis=0, concat_axis=0, axis...  34.2 us
    pallas_call x3, Pallas kernels, beam_stage(): pl.pallas_call(functools.partial(beam_kernel, start, frames, chans), out_...  31.8 us
    pallas_call x3, Pallas kernels, dft_stage(): pl.pallas_call(functools.partial(dft_kernel, frames, feeds), grid=(peers...  29.7 us
    unnamed x38, local copies, waits for them, and re-layouts  24.7 us
    all_to_all x3, starting transfers between devices, exchange(): lax.all_to_all(spectra, PEERS, split_axis=0, concat_axis=0, tiled=True)  16.1 us
    reshape x3, local copies, waits for them, and re-layouts, dft_stage(): volt = volt.reshape(feeds, length)  6.72 us
  transfers between devices with their start and end apart: 3, of which 2 were waited for; matrix products, arithmetic and copies ran while one was open for 5% of the time, Pallas kernels for 18%

profile of v3, /device:TPU:0, one launch (start us, length us, event | category | flops | bytes accessed | tf_op | source)
XLA Modules:
  0.0 277.0 jit_solution(776788660408650143)
XLA Ops:
  2.0 2.0 slice_bitcast_fusion.1.volt_ref
  4.6 2.7 fusion.table_ref
  7.3 8.1 %shard_map.65 = bf16[16,8,64,128]{3,2,1,0:T(8,128)(2,1)} custom-call(f32[4,2048]{1,0:T(4,128)S(1)} %fusion.34.window_ref, bf16[64,22528]{1,0:T(8,128)(2,1)S(1)} %slice_bitcast_fusion.1.volt_ref, bf16[2048,2048]{1,0:T(8,128)(2,1)S(1)} %fusion.table_ref), custom_call_target="tpu_custom_call" | custom-call | tf_op jit(solution)/shard_map/pallas_call | solution.py:107
  15.4 3.3 %copy-done.2 = bf16[2048,2048]{1,0:T(8,128)(2,1)} copy-done((bf16[2048,2048]{1,0:T(8,128)(2,1)}, bf16[2048,2048]{1,0:T(8,128)(2,1)S(1)}, u32[]{:S(2)}) %copy-start.2) | copy-done | bytes 8388632
  18.7 7.4 %all-to-all-start = ((bf16[16,8,64,128]{3,2,1,0:T(8,128)(2,1)}), bf16[16,8,64,128]{3,2,1,0:T(8,128)(2,1)S(1)}, u32[]{:S(2)}, u32[]{:S(2)}) async-start(bf16[16,8,64,128]{3,2,1,0:T(8,128)(2,1)} %shard_map.65), calls=%async_computation | async-start | bytes 4194304 | tf_op jit(solution)/shard_map/all_to_all | solution.py:234
  26.1 3.1 %slice_bitcast_fusion.volt_ref = bf16[64,47104]{1,0:T(8,128)(2,1)S(1)} fusion(bf16[64,1,71680]{2,0,1:T(8,128)(2,1)} %param.6), kind=kLoop, calls=%fused_computation.2 | loop fusion | bytes 12058624 | tf_op jit(solution)/shard_map/reshape | solution.py:95
  29.2 17.3 %shard_map.67 = bf16[16,20,64,128]{3,2,1,0:T(8,128)(2,1)S(1)} custom-call(f32[4,2048]{1,0:T(4,128)S(1)} %fusion.34.window_ref, bf16[64,47104]{1,0:T(8,128)(2,1)S(1)} %slice_bitcast_fusion.volt_ref, bf16[2048,2048]{1,0:T(8,128)(2,1)} %copy-done.2), custom_call_target="tpu_custom_call" | custom-call | tf_op jit(solution)/shard_map/pallas_call | solution.py:107
  46.5 2.4 copy-done.7
  48.9 26.5 %all-to-all-done.r_ref = bf16[16,8,64,128]{3,2,1,0:T(8,128)(2,1)S(1)} async-done(((bf16[16,8,64,128]{3,2,1,0:T(8,128)(2,1)}), bf16[16,8,64,128]{3,2,1,0:T(8,128)(2,1)S(1)}, u32[]{:S(2)}, u32[]{:S(2)}) %all-to-all-start) | async-done | bytes 2097184 | tf_op jit(solution)/shard_map/all_to_all | solution.py:234
  75.4 4.8 %all-to-all-start.2 = ((bf16[16,20,64,128]{3,2,1,0:T(8,128)(2,1)}), bf16[16,20,64,128]{3,2,1,0:T(8,128)(2,1)}, u32[]{:S(2)}, u32[]{:S(2)}) async-start(bf16[16,20,64,128]{3,2,1,0:T(8,128)(2,1)} %copy-done.7), calls=%async_computation.2 | async-start | bytes 10485760 | tf_op jit(solution)/shard_map/all_to_all | solution.py:234
  86.8 3.4 %copy-done.3 = bf16[2048,2048]{1,0:T(8,128)(2,1)S(1)} copy-done((bf16[2048,2048]{1,0:T(8,128)(2,1)S(1)}, bf16[2048,2048]{1,0:T(8,128)(2,1)}, u32[]{:S(2)}) %copy-start.3) | copy-done | bytes 8388632
  90.2 4.3 %shard_map.64 = bf16[16,4,64,128]{3,2,1,0:T(8,128)(2,1)S(1)} custom-call(f32[4,2048]{1,0:T(4,128)S(1)} %fusion.34.window_ref, bf16[64,14336]{1,0:T(8,128)(2,1)S(1)} %slice_bitcast_fusion.2.volt_ref, bf16[2048,2048]{1,0:T(8,128)(2,1)S(1)} %copy-done.3), custom_call_target="tpu_custom_call" | custom-call | tf_op jit(solution)/shard_map/pallas_call | solution.py:107
  99.1 7.7 %shard_map.66.rest_0_ = f32[1024,1024]{1,0:T(8,128)S(1)} custom-call(bf16[16,8,64,128]{3,2,1,0:T(8,128)(2,1)S(1)} %all-to-all-done.r_ref, f32[1024,128]{1,0:T(8,128)S(1)} %get-tuple-element.57.ga_ref, f32[1024,128]{1,0:T(8,128)S(1)} %get-tuple-element.58.gb_ref, bf16[1024,2048]{1,0:T(8,128)(2,1)S(1)} %bitcast.26, s32[64,1024]{1,0:T(8,128)S(1)} %add_select_fusion.1.e_ref), custom_call_target="tpu_custom_call" | custom-call | tf_op jit(solution)/shard_map/pallas_call | solution.py:198
  106.8 2.0 copy-done.4
  110.8 86.0 %all-to-all-done.2.r_ref = bf16[16,20,64,128]{3,2,1,0:T(8,128)(2,1)} async-done(((bf16[16,20,64,128]{3,2,1,0:T(8,128)(2,1)}), bf16[16,20,64,128]{3,2,1,0:T(8,128)(2,1)}, u32[]{:S(2)}, u32[]{:S(2)}) %all-to-all-start.2) | async-done | bytes 5242912 | tf_op jit(solution)/shard_map/all_to_all | solution.py:234
  196.7 3.9 %all-to-all-start.1 = ((bf16[16,4,64,128]{3,2,1,0:T(8,128)(2,1)}), bf16[16,4,64,128]{3,2,1,0:T(8,128)(2,1)S(1)}, u32[]{:S(2)}, u32[]{:S(2)}) async-start(bf16[16,4,64,128]{3,2,1,0:T(8,128)(2,1)} %copy-done.12), calls=%async_computation.1 | async-start | bytes 2097152 | tf_op jit(solution)/shard_map/all_to_all | solution.py:234
  200.7 2.2 copy-done.5
  202.8 2.2 copy-done.9
  205.0 20.6 %shard_map.68.rest_0_ = f32[1024,1024]{1,0:T(8,128)S(1)} custom-call(bf16[16,20,64,128]{3,2,1,0:T(8,128)(2,1)} %all-to-all-done.2.r_ref, f32[1024,128]{1,0:T(8,128)S(1)} %get-tuple-element.57.ga_ref, f32[1024,128]{1,0:T(8,128)S(1)} %get-tuple-element.58.gb_ref, bf16[1024,2048]{1,0:T(8,128)(2,1)S(1)} %bitcast.27, s32[64,1024]{1,0:T(8,128)S(1)} %add_select_fusion.1.e_ref, ...), custom_call_target="tpu_custom_call" | custom-call | tf_op jit(solution)/shard_map/pallas_call | solution.py:198
  227.6 2.2 copy-done.6
  229.8 2.2 copy-done.11
  232.0 3.5 %shard_map.69 = bf16[1024,1024]{1,0:T(8,128)(2,1)S(1)} custom-call(bf16[16,4,64,128]{3,2,1,0:T(8,128)(2,1)S(1)} %all-to-all-done.1.r_ref, f32[1024,128]{1,0:T(8,128)S(1)} %get-tuple-element.57.ga_ref, f32[1024,128]{1,0:T(8,128)S(1)} %get-tuple-element.58.gb_ref, bf16[1024,2048]{1,0:T(8,128)(2,1)S(1)} %bitcast.28, s32[64,1024]{1,0:T(8,128)S(1)} %add_select_fusion.1.e_ref, ...), custom_call_target="tpu_custom_call" | custom-call | tf_op jit(solution)/shard_map/pallas_call | solution.py:198
  235.5 5.5 %all_to_all.25 = bf16[2,512,1024]{2,1,0:T(8,128)(2,1)S(1)} all-to-all(bf16[2,512,1024]{2,1,0:T(8,128)(2,1)S(1)} %bitcast.29), channel_id=1, replica_groups={{0,8},{16,24},{1,9},{17,25},{2,10},{18,26},{3,11},{19,27},{4,12},{20,28..., dimensions={0} | all-to-all | bytes 4194304 | tf_op jit(solution)/shard_map/all_to_all | solution.py:285
  241.6 34.2 %all_to_all.26 = bf16[16,32,1024]{2,1,0:T(8,128)(2,1)S(1)} all-to-all(bf16[16,32,1024]{2,1,0:T(8,128)(2,1)S(1)} %bitcast.34), channel_id=1, replica_groups={{0,2,4,6,16,18,20,22,1,3,5,7,17,19,21,23},{8,10,12,14,24,26,28,30,9,11,..., dimensions={0} | all-to-all | bytes 2097152 | tf_op jit(solution)/shard_map/all_to_all | solution.py:299
  (73 shorter events, 19.2 us)
Async XLA Ops:
  0.0 80.3 %copy-start = (f32[64,2,256]{2,1,0:T(2,128)S(1)}, f32[64,2,256]{2,1,0:T(2,128)}, u32[]{:S(2)}) copy-start(f32[64,2,256]{2,1,0:T(2,128)} %param.7) | copy-start | bytes 393220
  15.4 3.3 %copy-start.2 = (bf16[2048,2048]{1,0:T(8,128)(2,1)}, bf16[2048,2048]{1,0:T(8,128)(2,1)S(1)}, u32[]{:S(2)}) copy-start(bf16[2048,2048]{1,0:T(8,128)(2,1)S(1)} %fusion.table_ref) | copy-start | bytes 25165828
  18.7 56.7 %all-to-all-start = ((bf16[16,8,64,128]{3,2,1,0:T(8,128)(2,1)}), bf16[16,8,64,128]{3,2,1,0:T(8,128)(2,1)S(1)}, u32[]{:S(2)}, u32[]{:S(2)}) async-start(bf16[16,8,64,128]{3,2,1,0:T(8,128)(2,1)} %shard_map.65), calls=%async_computation | async-start | bytes 4194304 | tf_op jit(solution)/shard_map/all_to_all | solution.py:234
  46.5 2.4 copy-start.7
  48.8 31.7 %copy-start.18 = (s32[1024]{0:T(1024)S(1)}, s32[1024]{0:T(1024)}, u32[]{:S(2)}) copy-start(s32[1024]{0:T(1024)} %param.9) | copy-start | bytes 12292
  48.9 35.2 %copy-start.17 = (s32[32,1024]{1,0:T(8,128)S(1)}, s32[32,1024]{1,0:T(8,128)}, u32[]{:S(2)}) copy-start(s32[32,1024]{1,0:T(8,128)} %param.10) | copy-start | bytes 393220
  75.4 121.4 %all-to-all-start.2 = ((bf16[16,20,64,128]{3,2,1,0:T(8,128)(2,1)}), bf16[16,20,64,128]{3,2,1,0:T(8,128)(2,1)}, u32[]{:S(2)}, u32[]{:S(2)}) async-start(bf16[16,20,64,128]{3,2,1,0:T(8,128)(2,1)} %copy-done.7), calls=%async_computation.2 | async-start | bytes 10485760 | tf_op jit(solution)/shard_map/all_to_all | solution.py:234
  86.8 3.4 %copy-start.3 = (bf16[2048,2048]{1,0:T(8,128)(2,1)S(1)}, bf16[2048,2048]{1,0:T(8,128)(2,1)}, u32[]{:S(2)}) copy-start(bf16[2048,2048]{1,0:T(8,128)(2,1)} %copy-done.2) | copy-start | bytes 25165828
  90.2 5.3 %copy-start.16 = (s32[1024,2]{0,1:T(2,128)S(1)}, s32[1024,2]{0,1:T(2,128)}, u32[]{:S(2)}) copy-start(s32[1024,2]{0,1:T(2,128)} %param.8) | copy-start | bytes 24580
  94.6 1.0 copy-start.12
  95.5 1.1 copy-start.15
  95.5 1.4 copy-start.14
  96.2 1.0 copy-start.13
  106.8 2.0 copy-start.4
  108.8 2.0 copy-start.8
  196.7 30.9 %all-to-all-start.1 = ((bf16[16,4,64,128]{3,2,1,0:T(8,128)(2,1)}), bf16[16,4,64,128]{3,2,1,0:T(8,128)(2,1)S(1)}, u32[]{:S(2)}, u32[]{:S(2)}) async-start(bf16[16,4,64,128]{3,2,1,0:T(8,128)(2,1)} %copy-done.12), calls=%async_computation.1 | async-start | bytes 2097152 | tf_op jit(solution)/shard_map/all_to_all | solution.py:234
  200.6 2.2 copy-start.5
  202.8 2.2 copy-start.9
  225.7 2.0 copy-start.10
  227.6 2.2 copy-start.6
  229.8 2.2 copy-start.11
  235.5 41.5 %copy-start.1 = (f32[64,2,256]{2,1,0:T(2,128)S(1)}, f32[64,2,256]{2,1,0:T(2,128)}, u32[]{:S(2)}) copy-start(f32[64,2,256]{2,1,0:T(2,128)} %param.7) | copy-start | bytes 393220

commit v4 on v3

--- a/solution.py
+++ b/solution.py
@@ -69,7 +69,7 @@
 
 BEAM_VMEM = 40
 DFT_VMEM = 40
-CHUNKS = (8, 20, 4)
+CHUNKS = (4, 24, 4)
 
 
 def dft_kernel(frames, feeds, window_ref, volt_ref, table_ref, out_ref, framed_ref):
@@ -107,7 +107,7 @@
     return pl.pallas_call(
         functools.partial(dft_kernel, frames, feeds),
         grid=(peers // step,),
-        out_shape=jax.ShapeDtypeStruct((peers, frames, feeds, width), jnp.bfloat16),
+        out_shape=pltpu.HBM((peers, frames, feeds, width), jnp.bfloat16),
         in_specs=[
             pl.BlockSpec((TAPS, NFFT), lambda i: (0, 0)),
             pl.BlockSpec((feeds, length), lambda i: (0, 0)),

time: 278 us -> 279 us (level)
  waiting for transfers between devices: 112 us -> 115 us
    unnamed x38 -> x32, local copies, waits for them, and re-layouts: 24.7 us -> 21.3 us
    reshape x3 -> x2, local copies, waits for them, and re-layouts: 6.72 us -> 5.81 us  [dft_stage(): volt = volt.reshape(feeds, length)]
  transfers between devices with their start and end apart: 3 -> 3, of which waited for: 2 -> 2; matrix products, arithmetic and copies ran while one was open for 5% -> 5% of each run, Pallas kernels for 18% -> 20%
where the time goes in v4:
time: 279 us; the launch traced here: 278 us
  waiting for transfers between devices  115 us (41%)
  Pallas kernels  62.8 us (23%)
  blocking collectives  39.7 us (14%)
  local copies, waits for them, and re-layouts  32.8 us (12%)
  starting transfers between devices  16.2 us (6%)
  other arithmetic  10.7 us (4%)
    all_to_all x3, waiting for transfers between devices, exchange(): lax.all_to_all(spectra, PEERS, split_axis=0, concat_axis=0, tiled=True)  115 us
    all_to_all x1, blocking collectives, local(): lax.all_to_all(part, ('pair',) + PEERS, split_axis=0, concat_axis=0, axis...  34.2 us
    pallas_call x3, Pallas kernels, beam_stage(): pl.pallas_call(functools.partial(beam_kernel, start, frames, chans), out_...  31.5 us
    pallas_call x3, Pallas kernels, dft_stage(): pl.pallas_call(functools.partial(dft_kernel, frames, feeds), grid=(peers...  31.3 us
    unnamed x32, local copies, waits for them, and re-layouts  21.3 us
    all_to_all x3, starting transfers between devices, exchange(): lax.all_to_all(spectra, PEERS, split_axis=0, concat_axis=0, tiled=True)  16.2 us
    reshape x2, local copies, waits for them, and re-layouts, dft_stage(): volt = volt.reshape(feeds, length)  5.81 us
  transfers between devices with their start and end apart: 3, of which 2 were waited for; matrix products, arithmetic and copies ran while one was open for 5% of the time, Pallas kernels for 20%

profile of v4, /device:TPU:0, one launch (start us, length us, event | category | flops | bytes accessed | tf_op | source)
XLA Modules:
  0.0 278.0 jit_solution(9456877781487004606)
XLA Ops:
  2.6 2.3 slice_bitcast_fusion.1
  4.9 2.7 fusion.table_ref
  7.6 5.1 %shard_map.65 = bf16[16,4,64,128]{3,2,1,0:T(8,128)(2,1)} custom-call(f32[4,2048]{1,0:T(4,128)S(1)} %fusion.34.window_ref, bf16[64,14336]{1,0:T(8,128)(2,1)S(1)} %get-tuple-element.33.volt_ref, bf16[2048,2048]{1,0:T(8,128)(2,1)S(1)} %fusion.table_ref), custom_call_target="tpu_custom_call" | custom-call | tf_op jit(solution)/shard_map/pallas_call | solution.py:107
  12.7 3.2 %copy-done.2 = bf16[2048,2048]{1,0:T(8,128)(2,1)} copy-done((bf16[2048,2048]{1,0:T(8,128)(2,1)}, bf16[2048,2048]{1,0:T(8,128)(2,1)S(1)}, u32[]{:S(2)}) %copy-start.2) | copy-done | bytes 8388632
  15.9 7.4 %all-to-all-start = ((bf16[16,4,64,128]{3,2,1,0:T(8,128)(2,1)}), bf16[16,4,64,128]{3,2,1,0:T(8,128)(2,1)S(1)}, u32[]{:S(2)}, u32[]{:S(2)}) async-start(bf16[16,4,64,128]{3,2,1,0:T(8,128)(2,1)} %shard_map.65), calls=%async_computation | async-start | bytes 2097152 | tf_op jit(solution)/shard_map/all_to_all | solution.py:234
  23.3 3.5 %slice_bitcast_fusion.volt_ref = bf16[64,55296]{1,0:T(8,128)(2,1)S(1)} fusion(bf16[64,1,71680]{2,0,1:T(8,128)(2,1)} %param.6), kind=kLoop, calls=%fused_computation.2 | loop fusion | bytes 14155776 | tf_op jit(solution)/shard_map/reshape | solution.py:95
  26.7 21.2 %shard_map.67 = bf16[16,24,64,128]{3,2,1,0:T(8,128)(2,1)} custom-call(f32[4,2048]{1,0:T(4,128)S(1)} %fusion.34.window_ref, bf16[64,55296]{1,0:T(8,128)(2,1)S(1)} %slice_bitcast_fusion.volt_ref, bf16[2048,2048]{1,0:T(8,128)(2,1)} %copy-done.2), custom_call_target="tpu_custom_call" | custom-call | tf_op jit(solution)/shard_map/pallas_call | solution.py:107
  48.0 2.1 all-to-all-done.r_ref
  50.1 4.8 %all-to-all-start.2 = ((bf16[16,24,64,128]{3,2,1,0:T(8,128)(2,1)}), bf16[16,24,64,128]{3,2,1,0:T(8,128)(2,1)}, u32[]{:S(2)}, u32[]{:S(2)}) async-start(bf16[16,24,64,128]{3,2,1,0:T(8,128)(2,1)} %shard_map.67), calls=%async_computation.2 | async-start | bytes 12582912 | tf_op jit(solution)/shard_map/all_to_all | solution.py:234
  61.8 3.4 %copy-done.3 = bf16[2048,2048]{1,0:T(8,128)(2,1)S(1)} copy-done((bf16[2048,2048]{1,0:T(8,128)(2,1)S(1)}, bf16[2048,2048]{1,0:T(8,128)(2,1)}, u32[]{:S(2)}) %copy-start.3) | copy-done | bytes 8388632
  65.2 5.0 %shard_map.64 = bf16[16,4,64,128]{3,2,1,0:T(8,128)(2,1)} custom-call(f32[4,2048]{1,0:T(4,128)S(1)} %fusion.34.window_ref, bf16[64,14336]{1,0:T(8,128)(2,1)S(1)} %get-tuple-element.34.volt_ref, bf16[2048,2048]{1,0:T(8,128)(2,1)S(1)} %copy-done.3), custom_call_target="tpu_custom_call" | custom-call | tf_op jit(solution)/shard_map/pallas_call | solution.py:107
  73.8 3.5 %shard_map.66.rest_0_ = f32[1024,1024]{1,0:T(8,128)S(1)} custom-call(bf16[16,4,64,128]{3,2,1,0:T(8,128)(2,1)S(1)} %all-to-all-done.r_ref, f32[1024,128]{1,0:T(8,128)S(1)} %get-tuple-element.59.ga_ref, f32[1024,128]{1,0:T(8,128)S(1)} %get-tuple-element.60.gb_ref, bf16[1024,2048]{1,0:T(8,128)(2,1)S(1)} %bitcast.26, s32[64,1024]{1,0:T(8,128)S(1)} %add_select_fusion.1.e_ref), custom_call_target="tpu_custom_call" | custom-call | tf_op jit(solution)/shard_map/pallas_call | solution.py:198
  77.3 1.9 copy-done.4
  79.3 2.0 copy-done.9
  81.3 112.7 %all-to-all-done.2.r_ref = bf16[16,24,64,128]{3,2,1,0:T(8,128)(2,1)} async-done(((bf16[16,24,64,128]{3,2,1,0:T(8,128)(2,1)}), bf16[16,24,64,128]{3,2,1,0:T(8,128)(2,1)}, u32[]{:S(2)}, u32[]{:S(2)}) %all-to-all-start.2) | async-done | bytes 6291488 | tf_op jit(solution)/shard_map/all_to_all | solution.py:234
  194.0 3.9 %all-to-all-start.1 = ((bf16[16,4,64,128]{3,2,1,0:T(8,128)(2,1)}), bf16[16,4,64,128]{3,2,1,0:T(8,128)(2,1)S(1)}, u32[]{:S(2)}, u32[]{:S(2)}) async-start(bf16[16,4,64,128]{3,2,1,0:T(8,128)(2,1)} %shard_map.64), calls=%async_computation.1 | async-start | bytes 2097152 | tf_op jit(solution)/shard_map/all_to_all | solution.py:234
  197.9 2.2 copy-done.5
  200.1 2.2 copy-done.10
  202.3 24.4 %shard_map.68.rest_0_ = f32[1024,1024]{1,0:T(8,128)S(1)} custom-call(bf16[16,24,64,128]{3,2,1,0:T(8,128)(2,1)} %all-to-all-done.2.r_ref, f32[1024,128]{1,0:T(8,128)S(1)} %get-tuple-element.59.ga_ref, f32[1024,128]{1,0:T(8,128)S(1)} %get-tuple-element.60.gb_ref, bf16[1024,2048]{1,0:T(8,128)(2,1)S(1)} %bitcast.27, s32[64,1024]{1,0:T(8,128)S(1)} %add_select_fusion.1.e_ref, ...), custom_call_target="tpu_custom_call" | custom-call | tf_op jit(solution)/shard_map/pallas_call | solution.py:198
  228.6 2.2 copy-done.6
  230.8 2.2 copy-done.8
  233.0 3.5 %shard_map.69 = bf16[1024,1024]{1,0:T(8,128)(2,1)S(1)} custom-call(bf16[16,4,64,128]{3,2,1,0:T(8,128)(2,1)S(1)} %all-to-all-done.1.r_ref, f32[1024,128]{1,0:T(8,128)S(1)} %get-tuple-element.59.ga_ref, f32[1024,128]{1,0:T(8,128)S(1)} %get-tuple-element.60.gb_ref, bf16[1024,2048]{1,0:T(8,128)(2,1)S(1)} %bitcast.28, s32[64,1024]{1,0:T(8,128)S(1)} %add_select_fusion.1.e_ref, ...), custom_call_target="tpu_custom_call" | custom-call | tf_op jit(solution)/shard_map/pallas_call | solution.py:198
  236.6 5.5 %all_to_all.25 = bf16[2,512,1024]{2,1,0:T(8,128)(2,1)S(1)} all-to-all(bf16[2,512,1024]{2,1,0:T(8,128)(2,1)S(1)} %bitcast.29), channel_id=1, replica_groups={{0,8},{16,24},{1,9},{17,25},{2,10},{18,26},{3,11},{19,27},{4,12},{20,28..., dimensions={0} | all-to-all | bytes 4194304 | tf_op jit(solution)/shard_map/all_to_all | solution.py:285
  242.7 34.2 %all_to_all.26 = bf16[16,32,1024]{2,1,0:T(8,128)(2,1)S(1)} all-to-all(bf16[16,32,1024]{2,1,0:T(8,128)(2,1)S(1)} %bitcast.34), channel_id=1, replica_groups={{0,2,4,6,16,18,20,22,1,3,5,7,17,19,21,23},{8,10,12,14,24,26,28,30,9,11,..., dimensions={0} | all-to-all | bytes 2097152 | tf_op jit(solution)/shard_map/all_to_all | solution.py:299
  (66 shorter events, 16.5 us)
Async XLA Ops:
  0.0 55.1 %copy-start = (f32[64,2,256]{2,1,0:T(2,128)S(1)}, f32[64,2,256]{2,1,0:T(2,128)}, u32[]{:S(2)}) copy-start(f32[64,2,256]{2,1,0:T(2,128)} %param.7) | copy-start | bytes 393220
  12.7 3.2 %copy-start.2 = (bf16[2048,2048]{1,0:T(8,128)(2,1)}, bf16[2048,2048]{1,0:T(8,128)(2,1)S(1)}, u32[]{:S(2)}) copy-start(bf16[2048,2048]{1,0:T(8,128)(2,1)S(1)} %fusion.table_ref) | copy-start | bytes 25165828
  15.9 34.2 %all-to-all-start = ((bf16[16,4,64,128]{3,2,1,0:T(8,128)(2,1)}), bf16[16,4,64,128]{3,2,1,0:T(8,128)(2,1)S(1)}, u32[]{:S(2)}, u32[]{:S(2)}) async-start(bf16[16,4,64,128]{3,2,1,0:T(8,128)(2,1)} %shard_map.65), calls=%async_computation | async-start | bytes 2097152 | tf_op jit(solution)/shard_map/all_to_all | solution.py:234
  48.0 7.3 %copy-start.15 = (s32[1024]{0:T(1024)S(1)}, s32[1024]{0:T(1024)}, u32[]{:S(2)}) copy-start(s32[1024]{0:T(1024)} %param.9) | copy-start | bytes 12292
  48.0 10.8 %copy-start.14 = (s32[32,1024]{1,0:T(8,128)S(1)}, s32[32,1024]{1,0:T(8,128)}, u32[]{:S(2)}) copy-start(s32[32,1024]{1,0:T(8,128)} %param.10) | copy-start | bytes 393220
  50.1 143.9 %all-to-all-start.2 = ((bf16[16,24,64,128]{3,2,1,0:T(8,128)(2,1)}), bf16[16,24,64,128]{3,2,1,0:T(8,128)(2,1)}, u32[]{:S(2)}, u32[]{:S(2)}) async-start(bf16[16,24,64,128]{3,2,1,0:T(8,128)(2,1)} %shard_map.67), calls=%async_computation.2 | async-start | bytes 12582912 | tf_op jit(solution)/shard_map/all_to_all | solution.py:234
  61.8 3.4 %copy-start.3 = (bf16[2048,2048]{1,0:T(8,128)(2,1)S(1)}, bf16[2048,2048]{1,0:T(8,128)(2,1)}, u32[]{:S(2)}) copy-start(bf16[2048,2048]{1,0:T(8,128)(2,1)} %copy-done.2) | copy-start | bytes 25165828
  65.2 5.0 %copy-start.13 = (s32[1024,2]{0,1:T(2,128)S(1)}, s32[1024,2]{0,1:T(2,128)}, u32[]{:S(2)}) copy-start(s32[1024,2]{0,1:T(2,128)} %param.8) | copy-start | bytes 24580
  70.2 1.0 copy-start.12
  70.2 1.4 copy-start.11
  77.3 2.0 copy-start.4
  79.3 2.0 copy-start.9
  194.0 34.7 %all-to-all-start.1 = ((bf16[16,4,64,128]{3,2,1,0:T(8,128)(2,1)}), bf16[16,4,64,128]{3,2,1,0:T(8,128)(2,1)S(1)}, u32[]{:S(2)}, u32[]{:S(2)}) async-start(bf16[16,4,64,128]{3,2,1,0:T(8,128)(2,1)} %shard_map.64), calls=%async_computation.1 | async-start | bytes 2097152 | tf_op jit(solution)/shard_map/all_to_all | solution.py:234
  197.9 2.2 copy-start.5
  200.1 2.2 copy-start.10
  226.7 1.9 copy-start.7
  228.6 2.2 copy-start.6
  230.8 2.2 copy-start.8
  236.5 41.5 %copy-start.1 = (f32[64,2,256]{2,1,0:T(2,128)S(1)}, f32[64,2,256]{2,1,0:T(2,128)}, u32[]{:S(2)}) copy-start(f32[64,2,256]{2,1,0:T(2,128)} %param.7) | copy-start | bytes 393220
